TPU v7x, 256 devices: a whole 4x4x8 slice. The times are simulated.
256 devices in a mesh: sec: 2 (over core), gx: 8 (over z), gy: 16 (over y, x).
Axes of the slice: x: 4, y: 4, z: 8, core: 2. Of those that a mesh axis runs over, the one named last changes fastest.
Arguments:
- air_sea_state: float32 [2, 16, 384, 4096], P('sec', None, 'gx', 'gy'), may hold values from -6 to 6
- diffusion: float32 [2, 16], P('sec'), may hold values from 0.04 to 0.15
- courant: float32 [2, 16], P('sec'), may hold values from 0.1 to 0.35
- exchange_coef: float32 [2, 384, 4096], P('sec', 'gx', 'gy'), may hold values from 0.2 to 1
- src_block: int32 [2, 24576], P('sec', ('gx', 'gy')), may hold values from 0 to 95
- dest_peer: int32 [2, 24576, 1], P('sec', ('gx', 'gy')), may hold values from 0 to 127; in each aligned block of 192 rows (0 to 191, 192 to 383, ..., all dimensions but the last counted through in order) at most 3 rows name the same one
- dest_block: int32 [2, 24576], P('sec', ('gx', 'gy')), may hold values from 0 to 95
- remap_weight: float32 [2, 24576, 128, 128], P('sec', ('gx', 'gy')), may hold values from -0.375 to 0.375
Outputs:
- new_state: float32 [2, 16, 384, 4096], P('sec', None, 'gx', 'gy')
- remapped: float32 [2, 4, 384, 4096], P('sec', None, 'gx', 'gy')
Inputs may be any that keep to these rules, and one draw needn't show every extreme that they name: `dest_peer`: among the 192 entries owned by one device (aligned blocks of 192 entries of one component), no destination device is named more than 3 times, and in every draw some device is named exactly 3 times by some owner.
All inputs are finite; a program needn't handle non-finite values.
Results may differ from a plain program's by a relative error of at most 0.0001.
Values sent between devices are 32-bit elements; how exact they have to be, the bound alone decides.
No kernel may reach another device: no remote copies, remote signals or barrier semaphores. Data moves between devices by JAX's collectives and lax.ppermute only.
A program may use at most 64 MiB of HBM per device.

v0:
```python
import jax
import jax.numpy as jnp
from jax import lax
from jax.sharding import PartitionSpec as P

NF = 4
BLK = 128
STEPS_A = 6
STEPS_O = 3


def swapped(block, axis, stride):
    count = lax.axis_size(axis)
    route = []
    for low in range(count):
        high = low | 1 << stride
        if high != low and high < count:
            route += [(low, high), (high, low)]
    return lax.ppermute(block, axis, route)


def padded_2(value, sides, width):
    for axis, dim in sides:
        count, length = (lax.axis_size(axis), value.shape[dim])
        up = [(i, (i + 1) % count) for i in range(count - 1)]
        down = [(j, i) for i, j in up]
        last = lax.slice_in_dim(value, length - width, length, axis=dim)
        initial = lax.slice_in_dim(value, 0, width, axis=dim)
        before = lax.ppermute(last, axis, up)
        after = lax.ppermute(initial, axis, down)
        value = jnp.concatenate([before, value, after], axis=dim)
    return value


def advance(levels, padded, diffuse, carry_rate):
    prev_x = padded[:, :-2, 1:-1]
    beside_all = padded[:, 2:, 1:-1] + prev_x + padded[:, 1:-1, 2:] + padded[:, 1:-1, :-2]
    return levels + diffuse * (beside_all - 4.0 * levels) - carry_rate * (levels - prev_x)


def remap_surface(surface, src_rows, target, dest_rows, weights):
    levels_n, rows_x, cols_y = surface.shape
    per_row = cols_y // BLK
    per_device = rows_x * per_row
    blocks = (
        surface.reshape(levels_n, rows_x, per_row, BLK)
        .transpose(1, 2, 0, 3)
        .reshape(per_device, levels_n, BLK)
    )
    picked = jnp.take(blocks, src_rows, axis=0)
    products = jnp.einsum("eij,efj->efi", weights, picked, precision=lax.Precision.HIGHEST)
    grid_x = lax.axis_size("gx")
    grid_y = lax.axis_size("gy")
    peer_count = grid_x * grid_y
    entries = weights.shape[0]
    capacity = max(2, 2 * entries // peer_count)
    total_slots = peer_count * capacity
    match_peer = (target[:, None] == jnp.arange(peer_count, dtype=jnp.int32)[None, :]).astype(
        jnp.int32
    )
    earlier = jnp.cumsum(match_peer, axis=0) - match_peer
    slot_index = jnp.sum(earlier * match_peer, axis=1)
    position = target * capacity + slot_index
    outgoing = jnp.zeros((total_slots, levels_n, BLK), jnp.float32).at[position].set(products)
    labels = jnp.full((total_slots,), -1, jnp.int32).at[position].set(dest_rows)
    incoming, labels_in = (
        lax.all_to_all(
            outgoing.reshape(peer_count, capacity, levels_n, BLK),
            ("gx", "gy"),
            split_axis=0,
            concat_axis=0,
            tiled=True,
        ),
        lax.all_to_all(
            labels.reshape(peer_count, capacity),
            ("gx", "gy"),
            split_axis=0,
            concat_axis=0,
            tiled=True,
        ),
    )
    incoming, labels_in = swapped((incoming, labels_in), "sec", 0)
    selector = (
        labels_in.reshape(total_slots)[:, None] == jnp.arange(per_device, dtype=jnp.int32)[None, :]
    ).astype(jnp.float32)
    summed = lax.dot_general(
        selector,
        incoming.reshape(total_slots, levels_n * BLK),
        (((0,), (0,)), ((), ())),
        precision=lax.Precision.HIGHEST,
    )
    return (
        summed.reshape(rows_x, per_row, levels_n, BLK)
        .transpose(2, 0, 1, 3)
        .reshape(levels_n, rows_x, cols_y)
    )


def body(
    air_sea_state, diffusion, courant, exchange_coef, src_block, dest_peer, dest_block, remap_weight
):
    section = lax.axis_index("sec")
    step_limit = jnp.where(section == 0, STEPS_A, STEPS_O)
    levels = air_sea_state[0]
    diffuse = diffusion[0][:, None, None]
    carry_rate = courant[0][:, None, None]
    src_rows = src_block[0]
    target = dest_peer[0][:, 0]
    dest_rows = dest_block[0]
    weights = remap_weight[0]
    for sweep_index in range(STEPS_A):
        padded = padded_2(levels, (("gx", 1), ("gy", 2)), 1)
        levels = jnp.where(
            sweep_index < step_limit, advance(levels, padded, diffuse, carry_rate), levels
        )
    surface = levels[:NF]
    remapped = remap_surface(surface, src_rows, target, dest_rows, weights)
    aloft = levels[NF:]
    coupling = exchange_coef[0][None]
    new_surface = surface + coupling * jnp.tanh(remapped - surface)
    new_state = jnp.concatenate([new_surface, aloft], axis=0)
    return (new_state[None], remapped[None])


def solution(mesh):
    in_specs = (
        P("sec", None, "gx", "gy"),
        P("sec", None),
        P("sec", None),
        P("sec", "gx", "gy"),
        P("sec", ("gx", "gy")),
        P("sec", ("gx", "gy"), None),
        P("sec", ("gx", "gy")),
        P("sec", ("gx", "gy"), None, None),
    )
    out_specs = (P("sec", None, "gx", "gy"), P("sec", None, "gx", "gy"))
    return jax.shard_map(body, mesh=mesh, in_specs=in_specs, out_specs=out_specs, check_vma=False)
```

profile of v0, /device:TPU:1, one launch (start us, length us, event | category | flops | bytes accessed | tf_op | source)
XLA Modules:
  0.0 244.5 jit_solution(3462629530854571554)
XLA Ops:
  3.0 5.0 %collective-permute-start.1 = (f32[16,1,256]{2,1,0:T(1,128)S(1)}, f32[16,1,256]{2,1,0:T(1,128)S(1)}, u32[]{:S(2)}, u32[]{:S(2)}) collective-permute-start(f32[16,1,256]{2,1,0:T(1,128)S(1)} %get-tuple-element.24), channel_id=1, source_target_pairs={{0,16},{16,32},{32,48},{48,64},{64,80},{80,96},{96,112},{1,17},{17... | collective-permute-start | bytes 49160 | tf_op jit(solution)/shard_map/ppermute | solution.py:29
  11.5 4.0 %collective-permute-start.3 = (f32[16,50,1]{2,1,0:T(8,128)S(1)}, f32[16,50,1]{2,1,0:T(8,128)S(1)}, u32[]{:S(2)}, u32[]{:S(2)}) collective-permute-start(f32[16,50,1]{2,1,0:T(8,128)S(1)} %get-tuple-element.13), channel_id=1, source_target_pairs={{0,1},{1,2},{2,3},{3,4},{4,5},{5,6},{6,7},{7,8},{8,9},{9,10},{10,1... | collective-permute-start | bytes 9608 | tf_op jit(solution)/shard_map/ppermute | solution.py:29
  15.6 5.2 %collective-permute-done.2 = f32[16,50,1]{2,1,0:T(8,128)S(1)} collective-permute-done((f32[16,50,1]{2,1,0:T(8,128)S(1)}, f32[16,50,1]{2,1,0:T(8,128)S(1)}, u32[]{:S(2)}, u32[]{:S(2)}) %collective-permute-start.2) | collective-permute-done | bytes 3232 | tf_op jit(solution)/shard_map/ppermute | solution.py:30
  21.7 3.5 %fusion.57 = f32[16,48,256]{2,1,0:T(8,128)S(1)} fusion(f32[16,48,256]{2,1,0:T(8,128)} %bitcast.68, f32[16,50,1]{2,1,0:T(8,128)S(1)} %collective-permute-done.3, f32[16,1,256]{2,1,0:T(1,128)S(1)} %collective-permute-done, f32[16,1,256]{2,1,0:T(1,128)S(1)} %collective-permute-done.1, f32[16,50,1]{2,1,0:T(8,128)S(1)} %collective-permute-done.2, ...), kind=kLoop, calls=%fused_computation.108 | loop fusion | flops 3735552 | bytes 1612161 | tf_op jit(solution)/shard_map/jit(_where)/select_n | solution.py:113
  26.5 4.0 %collective-permute-start.5 = (f32[16,1,256]{2,1,0:T(1,128)S(1)}, f32[16,1,256]{2,1,0:T(1,128)S(1)}, u32[]{:S(2)}, u32[]{:S(2)}) collective-permute-start(f32[16,1,256]{2,1,0:T(1,128)S(1)} %get-tuple-element.22), channel_id=1, source_target_pairs={{0,16},{16,32},{32,48},{48,64},{64,80},{80,96},{96,112},{1,17},{17... | collective-permute-start | bytes 49160 | tf_op jit(solution)/shard_map/ppermute | solution.py:29
  32.9 5.3 %collective-permute-start.7 = (f32[16,50,1]{2,1,0:T(8,128)S(1)}, f32[16,50,1]{2,1,0:T(8,128)S(1)}, u32[]{:S(2)}, u32[]{:S(2)}) collective-permute-start(f32[16,50,1]{2,1,0:T(8,128)S(1)} %get-tuple-element.11), channel_id=1, source_target_pairs={{0,1},{1,2},{2,3},{3,4},{4,5},{5,6},{6,7},{7,8},{8,9},{9,10},{10,1... | collective-permute-start | bytes 9608 | tf_op jit(solution)/shard_map/ppermute | solution.py:29
  38.2 3.9 %collective-permute-done.6 = f32[16,50,1]{2,1,0:T(8,128)S(1)} collective-permute-done((f32[16,50,1]{2,1,0:T(8,128)S(1)}, f32[16,50,1]{2,1,0:T(8,128)S(1)}, u32[]{:S(2)}, u32[]{:S(2)}) %collective-permute-start.6) | collective-permute-done | bytes 3232 | tf_op jit(solution)/shard_map/ppermute | solution.py:30
  42.1 1.5 collective-permute-done.7
  43.6 1.6 fusion.47
  46.5 5.4 %collective-permute-start.9 = (f32[16,1,256]{2,1,0:T(1,128)S(1)}, f32[16,1,256]{2,1,0:T(1,128)S(1)}, u32[]{:S(2)}, u32[]{:S(2)}) collective-permute-start(f32[16,1,256]{2,1,0:T(1,128)S(1)} %get-tuple-element.20), channel_id=1, source_target_pairs={{0,16},{16,32},{32,48},{48,64},{64,80},{80,96},{96,112},{1,17},{17... | collective-permute-start | bytes 49160 | tf_op jit(solution)/shard_map/ppermute | solution.py:29
  54.3 4.8 %collective-permute-start.11 = (f32[16,50,1]{2,1,0:T(8,128)S(1)}, f32[16,50,1]{2,1,0:T(8,128)S(1)}, u32[]{:S(2)}, u32[]{:S(2)}) collective-permute-start(f32[16,50,1]{2,1,0:T(8,128)S(1)} %get-tuple-element.9), channel_id=1, source_target_pairs={{0,1},{1,2},{2,3},{3,4},{4,5},{5,6},{6,7},{7,8},{8,9},{9,10},{10,1... | collective-permute-start | bytes 9608 | tf_op jit(solution)/shard_map/ppermute | solution.py:29
  59.1 3.8 %collective-permute-done.10 = f32[16,50,1]{2,1,0:T(8,128)S(1)} collective-permute-done((f32[16,50,1]{2,1,0:T(8,128)S(1)}, f32[16,50,1]{2,1,0:T(8,128)S(1)}, u32[]{:S(2)}, u32[]{:S(2)}) %collective-permute-start.10) | collective-permute-done | bytes 3232 | tf_op jit(solution)/shard_map/ppermute | solution.py:30
  63.0 1.5 collective-permute-done.11
  66.7 6.3 %collective-permute-start.13 = (f32[16,1,256]{2,1,0:T(1,128)S(1)}, f32[16,1,256]{2,1,0:T(1,128)S(1)}, u32[]{:S(2)}, u32[]{:S(2)}) collective-permute-start(f32[16,1,256]{2,1,0:T(1,128)S(1)} %get-tuple-element.18), channel_id=1, source_target_pairs={{0,16},{16,32},{32,48},{48,64},{64,80},{80,96},{96,112},{1,17},{17... | collective-permute-start | bytes 49160 | tf_op jit(solution)/shard_map/ppermute | solution.py:29
  75.5 4.8 %collective-permute-start.15 = (f32[16,50,1]{2,1,0:T(8,128)S(1)}, f32[16,50,1]{2,1,0:T(8,128)S(1)}, u32[]{:S(2)}, u32[]{:S(2)}) collective-permute-start(f32[16,50,1]{2,1,0:T(8,128)S(1)} %get-tuple-element.7), channel_id=1, source_target_pairs={{0,1},{1,2},{2,3},{3,4},{4,5},{5,6},{6,7},{7,8},{8,9},{9,10},{10,1... | collective-permute-start | bytes 9608 | tf_op jit(solution)/shard_map/ppermute | solution.py:29
  80.4 3.7 %collective-permute-done.14 = f32[16,50,1]{2,1,0:T(8,128)S(1)} collective-permute-done((f32[16,50,1]{2,1,0:T(8,128)S(1)}, f32[16,50,1]{2,1,0:T(8,128)S(1)}, u32[]{:S(2)}, u32[]{:S(2)}) %collective-permute-start.14) | collective-permute-done | bytes 3232 | tf_op jit(solution)/shard_map/ppermute | solution.py:30
  84.1 1.5 collective-permute-done.15
  86.5 1.3 collective-permute-start.16
  87.8 4.9 %collective-permute-start.17 = (f32[16,1,256]{2,1,0:T(1,128)S(1)}, f32[16,1,256]{2,1,0:T(1,128)S(1)}, u32[]{:S(2)}, u32[]{:S(2)}) collective-permute-start(f32[16,1,256]{2,1,0:T(1,128)S(1)} %get-tuple-element.16), channel_id=1, source_target_pairs={{0,16},{16,32},{32,48},{48,64},{64,80},{80,96},{96,112},{1,17},{17... | collective-permute-start | bytes 49160 | tf_op jit(solution)/shard_map/ppermute | solution.py:29
  95.2 5.7 %collective-permute-start.19 = (f32[16,50,1]{2,1,0:T(8,128)S(1)}, f32[16,50,1]{2,1,0:T(8,128)S(1)}, u32[]{:S(2)}, u32[]{:S(2)}) collective-permute-start(f32[16,50,1]{2,1,0:T(8,128)S(1)} %get-tuple-element.5), channel_id=1, source_target_pairs={{0,1},{1,2},{2,3},{3,4},{4,5},{5,6},{6,7},{7,8},{8,9},{9,10},{10,1... | collective-permute-start | bytes 9608 | tf_op jit(solution)/shard_map/ppermute | solution.py:29
  101.0 3.9 %collective-permute-done.18 = f32[16,50,1]{2,1,0:T(8,128)S(1)} collective-permute-done((f32[16,50,1]{2,1,0:T(8,128)S(1)}, f32[16,50,1]{2,1,0:T(8,128)S(1)}, u32[]{:S(2)}, u32[]{:S(2)}) %collective-permute-start.18) | collective-permute-done | bytes 3232 | tf_op jit(solution)/shard_map/ppermute | solution.py:30
  104.8 1.5 collective-permute-done.19
  108.6 5.2 %collective-permute-start.21 = (f32[16,1,256]{2,1,0:T(1,128)S(1)}, f32[16,1,256]{2,1,0:T(1,128)S(1)}, u32[]{:S(2)}, u32[]{:S(2)}) collective-permute-start(f32[16,1,256]{2,1,0:T(1,128)S(1)} %get-tuple-element.14), channel_id=1, source_target_pairs={{0,16},{16,32},{32,48},{48,64},{64,80},{80,96},{96,112},{1,17},{17... | collective-permute-start | bytes 49160 | tf_op jit(solution)/shard_map/ppermute | solution.py:29
  116.2 7.1 %collective-permute-start.23 = (f32[16,50,1]{2,1,0:T(8,128)S(1)}, f32[16,50,1]{2,1,0:T(8,128)S(1)}, u32[]{:S(2)}, u32[]{:S(2)}) collective-permute-start(f32[16,50,1]{2,1,0:T(8,128)S(1)} %get-tuple-element.3), channel_id=1, source_target_pairs={{0,1},{1,2},{2,3},{3,4},{4,5},{5,6},{6,7},{7,8},{8,9},{9,10},{10,1... | collective-permute-start | bytes 9608 | tf_op jit(solution)/shard_map/ppermute | solution.py:29
  123.3 3.7 %collective-permute-done.22 = f32[16,50,1]{2,1,0:T(8,128)S(1)} collective-permute-done((f32[16,50,1]{2,1,0:T(8,128)S(1)}, f32[16,50,1]{2,1,0:T(8,128)S(1)}, u32[]{:S(2)}, u32[]{:S(2)}) %collective-permute-start.22) | collective-permute-done | bytes 3232 | tf_op jit(solution)/shard_map/ppermute | solution.py:30
  127.0 1.5 collective-permute-done.23
  130.5 22.1 %fusion = f32[192,4,128]{2,1,0:T(4,128)S(1)} fusion(f32[1,192,128,128]{3,2,1,0:T(8,128)} %param.15, f32[192,4,128]{2,1,0:T(4,128)S(1)} %gather_fusion, pred[192]{0:T(512)(128)(4,1)S(1)} %compare_and_fusion), kind=kOutput, calls=%fused_computation.3 | convolution fusion | flops 151093248 | bytes 13369536 | tf_op jit(solution)/shard_map/eij,efj->efi/dot_general | solution.py:51
  152.8 6.2 %scatter_fusion = f32[384,4,128]{2,1,0:T(4,128)S(1)} fusion(f32[384,4,128]{2,1,0:T(4,128)S(1)} %broadcast_in_dim.24, s32[192]{0:T(256)S(1)} %bitcast.98, f32[192,4,128]{2,1,0:T(4,128)S(1)} %fusion), kind=kCustom, calls=%fused_computation.2 | custom fusion | bytes 1180416 | tf_op jit(solution)/shard_map/scatter | solution.py:64
  159.0 47.0 %all_to_all.17 = f32[128,3,4,128]{3,2,1,0:T(4,128)S(1)} all-to-all(f32[128,3,4,128]{3,2,1,0:T(4,128)S(1)} %bitcast.65), channel_id=1, replica_groups=mesh['sec'=2,'gx'=8,'gy'=16] {'gx','gy'}, dimensions={0} | all-to-all | bytes 1572864 | tf_op jit(solution)/shard_map/all_to_all | solution.py:67
  206.0 15.2 %collective-permute-start.25 = (f32[128,3,4,128]{3,2,1,0:T(4,128)S(1)}, f32[128,3,4,128]{3,2,1,0:T(4,128)S(1)}, u32[]{:S(2)}, u32[]{:S(2)}) collective-permute-start(f32[128,3,4,128]{3,2,1,0:T(4,128)S(1)} %all_to_all.17), channel_id=1, source_target_pairs={{0,128},{128,0},{1,129},{129,1},{2,130},{130,2},{3,131},{131,3},{4... | collective-permute-start | bytes 2359304 | tf_op jit(solution)/shard_map/ppermute | solution.py:19
  221.2 1.3 scatter_custom_fusion
  222.7 16.6 %all_to_all.18 = s32[128,1,3]{2,1,0:T(1,128)S(1)} all-to-all(s32[128,1,3]{2,1,0:T(1,128)S(1)} %bitcast.78), channel_id=1, replica_groups=mesh['sec'=2,'gx'=8,'gy'=16] {'gx','gy'}, dimensions={0} | all-to-all | bytes 3072 | tf_op jit(solution)/shard_map/all_to_all | solution.py:74
  (89 shorter events, 34.5 us)
Async XLA Ops:
  0.6 63.8 %copy-start.2 = (f32[1,16]{1,0:T(1,128)S(1)}, f32[1,16]{1,0:T(1,128)}, u32[]{:S(2)}) copy-start(f32[1,16]{1,0:T(1,128)} %param.9) | copy-start | bytes 196
  0.6 63.8 %copy-start.1 = (f32[1,16]{1,0:T(1,128)S(1)}, f32[1,16]{1,0:T(1,128)}, u32[]{:S(2)}) copy-start(f32[1,16]{1,0:T(1,128)} %param.10) | copy-start | bytes 196
  0.7 79.6 %copy-start.3 = (s32[1,192,1]{1,2,0:T(1,128)S(1)}, s32[1,192,1]{1,2,0:T(1,128)}, u32[]{:S(2)}) copy-start(s32[1,192,1]{1,2,0:T(1,128)} %param.13) | copy-start | bytes 2308
  1.7 6.3 %collective-permute-start = (f32[16,1,256]{2,1,0:T(1,128)S(1)}, f32[16,1,256]{2,1,0:T(1,128)S(1)}, u32[]{:S(2)}, u32[]{:S(2)}) collective-permute-start(f32[16,1,256]{2,1,0:T(1,128)S(1)} %get-tuple-element.25), channel_id=1, source_target_pairs={{16,0},{32,16},{48,32},{64,48},{80,64},{96,80},{112,96},{17,1},{33... | collective-permute-start | bytes 49160 | tf_op jit(solution)/shard_map/ppermute | solution.py:30
  3.0 5.9 %collective-permute-start.1 = (f32[16,1,256]{2,1,0:T(1,128)S(1)}, f32[16,1,256]{2,1,0:T(1,128)S(1)}, u32[]{:S(2)}, u32[]{:S(2)}) collective-permute-start(f32[16,1,256]{2,1,0:T(1,128)S(1)} %get-tuple-element.24), channel_id=1, source_target_pairs={{0,16},{16,32},{32,48},{48,64},{64,80},{80,96},{96,112},{1,17},{17... | collective-permute-start | bytes 49160 | tf_op jit(solution)/shard_map/ppermute | solution.py:29
  10.2 10.5 %collective-permute-start.2 = (f32[16,50,1]{2,1,0:T(8,128)S(1)}, f32[16,50,1]{2,1,0:T(8,128)S(1)}, u32[]{:S(2)}, u32[]{:S(2)}) collective-permute-start(f32[16,50,1]{2,1,0:T(8,128)S(1)} %get-tuple-element.12), channel_id=1, source_target_pairs={{1,0},{2,1},{3,2},{4,3},{5,4},{6,5},{7,6},{8,7},{9,8},{10,9},{11,1... | collective-permute-start | bytes 9608 | tf_op jit(solution)/shard_map/ppermute | solution.py:30
  11.5 10.1 %collective-permute-start.3 = (f32[16,50,1]{2,1,0:T(8,128)S(1)}, f32[16,50,1]{2,1,0:T(8,128)S(1)}, u32[]{:S(2)}, u32[]{:S(2)}) collective-permute-start(f32[16,50,1]{2,1,0:T(8,128)S(1)} %get-tuple-element.13), channel_id=1, source_target_pairs={{0,1},{1,2},{2,3},{3,4},{4,5},{5,6},{6,7},{7,8},{8,9},{9,10},{10,1... | collective-permute-start | bytes 9608 | tf_op jit(solution)/shard_map/ppermute | solution.py:29
  21.7 79.2 %copy-start.4 = (s32[1,192]{1,0:T(1,128)S(1)}, s32[1,192]{1,0:T(1,128)}, u32[]{:S(2)}) copy-start(s32[1,192]{1,0:T(1,128)} %param.12) | copy-start | bytes 2308
  25.2 6.1 %collective-permute-start.4 = (f32[16,1,256]{2,1,0:T(1,128)S(1)}, f32[16,1,256]{2,1,0:T(1,128)S(1)}, u32[]{:S(2)}, u32[]{:S(2)}) collective-permute-start(f32[16,1,256]{2,1,0:T(1,128)S(1)} %get-tuple-element.23), channel_id=1, source_target_pairs={{16,0},{32,16},{48,32},{64,48},{80,64},{96,80},{112,96},{17,1},{33... | collective-permute-start | bytes 49160 | tf_op jit(solution)/shard_map/ppermute | solution.py:30
  26.5 4.8 %collective-permute-start.5 = (f32[16,1,256]{2,1,0:T(1,128)S(1)}, f32[16,1,256]{2,1,0:T(1,128)S(1)}, u32[]{:S(2)}, u32[]{:S(2)}) collective-permute-start(f32[16,1,256]{2,1,0:T(1,128)S(1)} %get-tuple-element.22), channel_id=1, source_target_pairs={{0,16},{16,32},{32,48},{48,64},{64,80},{80,96},{96,112},{1,17},{17... | collective-permute-start | bytes 49160 | tf_op jit(solution)/shard_map/ppermute | solution.py:29
  31.6 10.5 %collective-permute-start.6 = (f32[16,50,1]{2,1,0:T(8,128)S(1)}, f32[16,50,1]{2,1,0:T(8,128)S(1)}, u32[]{:S(2)}, u32[]{:S(2)}) collective-permute-start(f32[16,50,1]{2,1,0:T(8,128)S(1)} %get-tuple-element.10), channel_id=1, source_target_pairs={{1,0},{2,1},{3,2},{4,3},{5,4},{6,5},{7,6},{8,7},{9,8},{10,9},{11,1... | collective-permute-start | bytes 9608 | tf_op jit(solution)/shard_map/ppermute | solution.py:30
  32.9 10.6 %collective-permute-start.7 = (f32[16,50,1]{2,1,0:T(8,128)S(1)}, f32[16,50,1]{2,1,0:T(8,128)S(1)}, u32[]{:S(2)}, u32[]{:S(2)}) collective-permute-start(f32[16,50,1]{2,1,0:T(8,128)S(1)} %get-tuple-element.11), channel_id=1, source_target_pairs={{0,1},{1,2},{2,3},{3,4},{4,5},{5,6},{6,7},{7,8},{8,9},{9,10},{10,1... | collective-permute-start | bytes 9608 | tf_op jit(solution)/shard_map/ppermute | solution.py:29
  45.2 6.8 %collective-permute-start.8 = (f32[16,1,256]{2,1,0:T(1,128)S(1)}, f32[16,1,256]{2,1,0:T(1,128)S(1)}, u32[]{:S(2)}, u32[]{:S(2)}) collective-permute-start(f32[16,1,256]{2,1,0:T(1,128)S(1)} %get-tuple-element.21), channel_id=1, source_target_pairs={{16,0},{32,16},{48,32},{64,48},{80,64},{96,80},{112,96},{17,1},{33... | collective-permute-start | bytes 49160 | tf_op jit(solution)/shard_map/ppermute | solution.py:30
  46.5 6.2 %collective-permute-start.9 = (f32[16,1,256]{2,1,0:T(1,128)S(1)}, f32[16,1,256]{2,1,0:T(1,128)S(1)}, u32[]{:S(2)}, u32[]{:S(2)}) collective-permute-start(f32[16,1,256]{2,1,0:T(1,128)S(1)} %get-tuple-element.20), channel_id=1, source_target_pairs={{0,16},{16,32},{32,48},{48,64},{64,80},{80,96},{96,112},{1,17},{17... | collective-permute-start | bytes 49160 | tf_op jit(solution)/shard_map/ppermute | solution.py:29
  53.0 10.0 %collective-permute-start.10 = (f32[16,50,1]{2,1,0:T(8,128)S(1)}, f32[16,50,1]{2,1,0:T(8,128)S(1)}, u32[]{:S(2)}, u32[]{:S(2)}) collective-permute-start(f32[16,50,1]{2,1,0:T(8,128)S(1)} %get-tuple-element.8), channel_id=1, source_target_pairs={{1,0},{2,1},{3,2},{4,3},{5,4},{6,5},{7,6},{8,7},{9,8},{10,9},{11,1... | collective-permute-start | bytes 9608 | tf_op jit(solution)/shard_map/ppermute | solution.py:30
  54.3 10.2 %collective-permute-start.11 = (f32[16,50,1]{2,1,0:T(8,128)S(1)}, f32[16,50,1]{2,1,0:T(8,128)S(1)}, u32[]{:S(2)}, u32[]{:S(2)}) collective-permute-start(f32[16,50,1]{2,1,0:T(8,128)S(1)} %get-tuple-element.9), channel_id=1, source_target_pairs={{0,1},{1,2},{2,3},{3,4},{4,5},{5,6},{6,7},{7,8},{8,9},{9,10},{10,1... | collective-permute-start | bytes 9608 | tf_op jit(solution)/shard_map/ppermute | solution.py:29
  65.4 7.6 %collective-permute-start.12 = (f32[16,1,256]{2,1,0:T(1,128)S(1)}, f32[16,1,256]{2,1,0:T(1,128)S(1)}, u32[]{:S(2)}, u32[]{:S(2)}) collective-permute-start(f32[16,1,256]{2,1,0:T(1,128)S(1)} %get-tuple-element.19), channel_id=1, source_target_pairs={{16,0},{32,16},{48,32},{64,48},{80,64},{96,80},{112,96},{17,1},{33... | collective-permute-start | bytes 49160 | tf_op jit(solution)/shard_map/ppermute | solution.py:30
  66.7 7.1 %collective-permute-start.13 = (f32[16,1,256]{2,1,0:T(1,128)S(1)}, f32[16,1,256]{2,1,0:T(1,128)S(1)}, u32[]{:S(2)}, u32[]{:S(2)}) collective-permute-start(f32[16,1,256]{2,1,0:T(1,128)S(1)} %get-tuple-element.18), channel_id=1, source_target_pairs={{0,16},{16,32},{32,48},{48,64},{64,80},{80,96},{96,112},{1,17},{17... | collective-permute-start | bytes 49160 | tf_op jit(solution)/shard_map/ppermute | solution.py:29
  74.2 10.0 %collective-permute-start.14 = (f32[16,50,1]{2,1,0:T(8,128)S(1)}, f32[16,50,1]{2,1,0:T(8,128)S(1)}, u32[]{:S(2)}, u32[]{:S(2)}) collective-permute-start(f32[16,50,1]{2,1,0:T(8,128)S(1)} %get-tuple-element.6), channel_id=1, source_target_pairs={{1,0},{2,1},{3,2},{4,3},{5,4},{6,5},{7,6},{8,7},{9,8},{10,9},{11,1... | collective-permute-start | bytes 9608 | tf_op jit(solution)/shard_map/ppermute | solution.py:30
  75.5 10.1 %collective-permute-start.15 = (f32[16,50,1]{2,1,0:T(8,128)S(1)}, f32[16,50,1]{2,1,0:T(8,128)S(1)}, u32[]{:S(2)}, u32[]{:S(2)}) collective-permute-start(f32[16,50,1]{2,1,0:T(8,128)S(1)} %get-tuple-element.7), channel_id=1, source_target_pairs={{0,1},{1,2},{2,3},{3,4},{4,5},{5,6},{6,7},{7,8},{8,9},{9,10},{10,1... | collective-permute-start | bytes 9608 | tf_op jit(solution)/shard_map/ppermute | solution.py:29
  86.5 6.2 %collective-permute-start.16 = (f32[16,1,256]{2,1,0:T(1,128)S(1)}, f32[16,1,256]{2,1,0:T(1,128)S(1)}, u32[]{:S(2)}, u32[]{:S(2)}) collective-permute-start(f32[16,1,256]{2,1,0:T(1,128)S(1)} %get-tuple-element.17), channel_id=1, source_target_pairs={{16,0},{32,16},{48,32},{64,48},{80,64},{96,80},{112,96},{17,1},{33... | collective-permute-start | bytes 49160 | tf_op jit(solution)/shard_map/ppermute | solution.py:30
  87.8 5.8 %collective-permute-start.17 = (f32[16,1,256]{2,1,0:T(1,128)S(1)}, f32[16,1,256]{2,1,0:T(1,128)S(1)}, u32[]{:S(2)}, u32[]{:S(2)}) collective-permute-start(f32[16,1,256]{2,1,0:T(1,128)S(1)} %get-tuple-element.16), channel_id=1, source_target_pairs={{0,16},{16,32},{32,48},{48,64},{64,80},{80,96},{96,112},{1,17},{17... | collective-permute-start | bytes 49160 | tf_op jit(solution)/shard_map/ppermute | solution.py:29
  93.9 10.9 %collective-permute-start.18 = (f32[16,50,1]{2,1,0:T(8,128)S(1)}, f32[16,50,1]{2,1,0:T(8,128)S(1)}, u32[]{:S(2)}, u32[]{:S(2)}) collective-permute-start(f32[16,50,1]{2,1,0:T(8,128)S(1)} %get-tuple-element.4), channel_id=1, source_target_pairs={{1,0},{2,1},{3,2},{4,3},{5,4},{6,5},{7,6},{8,7},{9,8},{10,9},{11,1... | collective-permute-start | bytes 9608 | tf_op jit(solution)/shard_map/ppermute | solution.py:30
  95.2 11.1 %collective-permute-start.19 = (f32[16,50,1]{2,1,0:T(8,128)S(1)}, f32[16,50,1]{2,1,0:T(8,128)S(1)}, u32[]{:S(2)}, u32[]{:S(2)}) collective-permute-start(f32[16,50,1]{2,1,0:T(8,128)S(1)} %get-tuple-element.5), channel_id=1, source_target_pairs={{0,1},{1,2},{2,3},{3,4},{4,5},{5,6},{6,7},{7,8},{8,9},{9,10},{10,1... | collective-permute-start | bytes 9608 | tf_op jit(solution)/shard_map/ppermute | solution.py:29
  107.3 6.5 %collective-permute-start.20 = (f32[16,1,256]{2,1,0:T(1,128)S(1)}, f32[16,1,256]{2,1,0:T(1,128)S(1)}, u32[]{:S(2)}, u32[]{:S(2)}) collective-permute-start(f32[16,1,256]{2,1,0:T(1,128)S(1)} %get-tuple-element.15), channel_id=1, source_target_pairs={{16,0},{32,16},{48,32},{64,48},{80,64},{96,80},{112,96},{17,1},{33... | collective-permute-start | bytes 49160 | tf_op jit(solution)/shard_map/ppermute | solution.py:30
  108.6 6.1 %collective-permute-start.21 = (f32[16,1,256]{2,1,0:T(1,128)S(1)}, f32[16,1,256]{2,1,0:T(1,128)S(1)}, u32[]{:S(2)}, u32[]{:S(2)}) collective-permute-start(f32[16,1,256]{2,1,0:T(1,128)S(1)} %get-tuple-element.14), channel_id=1, source_target_pairs={{0,16},{16,32},{32,48},{48,64},{64,80},{80,96},{96,112},{1,17},{17... | collective-permute-start | bytes 49160 | tf_op jit(solution)/shard_map/ppermute | solution.py:29
  114.9 12.1 %collective-permute-start.22 = (f32[16,50,1]{2,1,0:T(8,128)S(1)}, f32[16,50,1]{2,1,0:T(8,128)S(1)}, u32[]{:S(2)}, u32[]{:S(2)}) collective-permute-start(f32[16,50,1]{2,1,0:T(8,128)S(1)} %get-tuple-element.2), channel_id=1, source_target_pairs={{1,0},{2,1},{3,2},{4,3},{5,4},{6,5},{7,6},{8,7},{9,8},{10,9},{11,1... | collective-permute-start | bytes 9608 | tf_op jit(solution)/shard_map/ppermute | solution.py:30
  116.2 12.3 %collective-permute-start.23 = (f32[16,50,1]{2,1,0:T(8,128)S(1)}, f32[16,50,1]{2,1,0:T(8,128)S(1)}, u32[]{:S(2)}, u32[]{:S(2)}) collective-permute-start(f32[16,50,1]{2,1,0:T(8,128)S(1)} %get-tuple-element.3), channel_id=1, source_target_pairs={{0,1},{1,2},{2,3},{3,4},{4,5},{5,6},{6,7},{7,8},{8,9},{9,10},{10,1... | collective-permute-start | bytes 9608 | tf_op jit(solution)/shard_map/ppermute | solution.py:29
  129.4 113.2 %copy-start = (f32[1,48,256]{2,1,0:T(8,128)S(1)}, f32[1,48,256]{2,1,0:T(8,128)}, u32[]{:S(2)}) copy-start(f32[1,48,256]{2,1,0:T(8,128)} %param.11) | copy-start | bytes 147460
  206.0 35.7 %collective-permute-start.25 = (f32[128,3,4,128]{3,2,1,0:T(4,128)S(1)}, f32[128,3,4,128]{3,2,1,0:T(4,128)S(1)}, u32[]{:S(2)}, u32[]{:S(2)}) collective-permute-start(f32[128,3,4,128]{3,2,1,0:T(4,128)S(1)} %all_to_all.17), channel_id=1, source_target_pairs={{0,128},{128,0},{1,129},{129,1},{2,130},{130,2},{3,131},{131,3},{4... | collective-permute-start | bytes 2359304 | tf_op jit(solution)/shard_map/ppermute | solution.py:19
  239.4 2.0 collective-permute-start.24
where the time goes:
time: 245 us
  starting transfers between devices  94.2 us (38%)
  blocking collectives  63.6 us (26%)
  waiting for transfers between devices  37.5 us (15%)
  matrix products  22.7 us (9%)
  local copies, waits for them, and re-layouts  12.8 us (5%)
  other arithmetic  12.5 us (5%)
    ppermute x12, starting transfers between devices, padded_2(): before = lax.ppermute(last, axis, up)  62.3 us
    all_to_all x1, blocking collectives, remap_surface(): lax.all_to_all(outgoing.reshape(peer_count, capacity, levels_n, BLK), ('g...  47 us
    ppermute x12, waiting for transfers between devices, padded_2(): after = lax.ppermute(initial, axis, down)  24.2 us
    dot_general x1, matrix products, remap_surface(): jnp.einsum('eij,efj->efi', weights, picked, precision=lax.Precision.HIGHEST)  22.1 us
    all_to_all x1, blocking collectives, remap_surface(): lax.all_to_all(labels.reshape(peer_count, capacity), ('gx', 'gy'), split_...  16.6 us
    ppermute x2, starting transfers between devices, swapped(): return lax.ppermute(block, axis, route)  16.3 us
    ppermute x12, starting transfers between devices, padded_2(): after = lax.ppermute(initial, axis, down)  15.5 us
    ppermute x12, waiting for transfers between devices, padded_2(): before = lax.ppermute(last, axis, up)  12.3 us
  transfers between devices with their start and end apart: 26, of which 19 were waited for; matrix products, arithmetic and copies ran while one was open for 1% of the time, Pallas kernels for 0%

commit v1 on v0

v1 whole, which is shorter than its diff:
```python
import jax
import jax.numpy as jnp
from jax import lax
from jax.experimental import pallas as pl
from jax.experimental.pallas import tpu as pltpu
from jax.sharding import PartitionSpec as P

LEV = 16
NF = 4
BLK = 128
CX = 48
CY = 256
BPD = 96
EPD = 192
CAP = 3
STEPS_A = 6
STEPS_O = 3
HALO = 8
ROWS = CX + 2 * HALO
COLS = CY + BLK
CHUNK = 16
N_CHUNKS = EPD // CHUNK


def ring(axis, shift):
    count = lax.axis_size(axis)
    return [(i, (i + shift) % count) for i in range(count)]


def inside(meta_ref):
    row = lax.broadcasted_iota(jnp.int32, (ROWS, COLS), 0)
    col = lax.broadcasted_iota(jnp.int32, (ROWS, COLS), 1)
    row = jnp.where(row >= CX + HALO, row - ROWS, row) + meta_ref[0]
    col = jnp.where(col >= CY + BLK // 2, col - COLS, col) + meta_ref[1]
    return (row >= 0) & (row < meta_ref[2]) & (col >= 0) & (col < meta_ref[3])


def extended(tile, top, bottom, from_left, from_right, level):
    lane = lax.broadcasted_iota(jnp.int32, (ROWS, BLK), 1)
    after = pltpu.roll(from_right, (BLK - HALO * level) % BLK, 1)
    before = pltpu.roll(from_left, (2 * BLK - HALO - HALO * level) % BLK, 1)
    beyond = jnp.where(lane < HALO, after, jnp.where(lane >= BLK - HALO, before, 0.0))
    own = jnp.concatenate([tile, bottom, top], axis=0)
    return jnp.concatenate([own, beyond], axis=1)


def evolve(field, keep, diffuse, carry_rate, steps):
    field = field * keep
    centre = 1.0 - 4.0 * diffuse - carry_rate
    upwind = diffuse + carry_rate

    def step(_, u):
        beside = pltpu.roll(u, ROWS - 1, 0) + pltpu.roll(u, 1, 1) + pltpu.roll(u, COLS - 1, 1)
        return (centre * u + upwind * pltpu.roll(u, 1, 0) + diffuse * beside) * keep

    return lax.fori_loop(0, steps, step, field)


def pack_kernel(x_ref, top_ref, bottom_ref, left_ref, right_ref):
    lane = lax.broadcasted_iota(jnp.int32, (ROWS, BLK), 1) // HALO
    left = jnp.zeros((ROWS, BLK), jnp.float32)
    right = jnp.zeros((ROWS, BLK), jnp.float32)
    for level in range(LEV):
        own = jnp.concatenate([x_ref[level], bottom_ref[level], top_ref[level]], axis=0)
        left = jnp.where(lane == level, pltpu.roll(own[:, :BLK], HALO * level, 1), left)
        right = jnp.where(
            lane == level, pltpu.roll(own[:, CY - BLK :], (HALO * level + HALO) % BLK, 1), right
        )
    left_ref[...] = left
    right_ref[...] = right


def surface_kernel(
    meta_ref, rates_ref, route_ref, x_ref, top_ref, bottom_ref, left_ref, right_ref, w_ref,
    slots_ref, surface_ref, w_buf, blocks, keep_ref, sems,
):
    def fetch(part):
        rows = pl.ds(part * CHUNK, CHUNK)
        return pltpu.make_async_copy(w_ref.at[rows], w_buf.at[rows], sems.at[part])

    for part in range(N_CHUNKS):
        fetch(part).start()
    slots_ref[...] = jnp.zeros(slots_ref.shape, jnp.float32)
    keep_ref[...] = inside(meta_ref).astype(jnp.float32)
    for level in range(NF):
        field = extended(
            x_ref[level], top_ref[level], bottom_ref[level], left_ref[...], right_ref[...], level
        )
        field = evolve(field, keep_ref[...], rates_ref[0, level], rates_ref[1, level], meta_ref[4])
        field = field[:CX, :CY]
        surface_ref[level] = field
        high = field.astype(jnp.bfloat16).astype(jnp.float32)
        low = field - high
        for half in range(2):
            cols = slice(half * BLK, (half + 1) * BLK)
            blocks[pl.ds(half * 8 + level, CX, stride=16), :] = high[:, cols]
            blocks[pl.ds(half * 8 + NF + level, CX, stride=16), :] = low[:, cols]

    def entry(e):
        picked = blocks[pl.ds(pl.multiple_of(route_ref[0, e] * 8, 8), 8), :].astype(jnp.bfloat16)
        weight = w_buf[e]
        high = weight.astype(jnp.bfloat16)
        low = (weight - high.astype(jnp.float32)).astype(jnp.bfloat16)
        dims = (((1,), (1,)), ((), ()))
        both = lax.dot_general(picked, high, dims, preferred_element_type=jnp.float32)
        both += lax.dot_general(picked, low, dims, preferred_element_type=jnp.float32)
        slots_ref[route_ref[1, e]] = both[:NF] + both[NF:]

    @pl.loop(0, N_CHUNKS)
    def _(part):
        fetch(part).wait()
        for k in range(CHUNK):
            entry(part * CHUNK + k)


def aloft_kernel(
    meta_ref, rates_ref, x_ref, top_ref, bottom_ref, left_ref, right_ref, out_ref, keep_ref
):
    group = pl.program_id(0) + 1

    @pl.when(group == 1)
    def _():
        keep_ref[...] = inside(meta_ref).astype(jnp.float32)

    for k in range(NF):
        level = group * NF + k
        field = extended(
            x_ref[k], top_ref[k], bottom_ref[k], left_ref[...], right_ref[...], level
        )
        field = evolve(field, keep_ref[...], rates_ref[0, level], rates_ref[1, level], meta_ref[4])
        out_ref[k] = field[:CX, :CY]


def finish_kernel(slots_ref, labels_ref, surface_ref, coef_ref, aloft_ref, state_ref, remapped_ref):
    del aloft_ref
    row = lax.broadcasted_iota(jnp.int32, (BPD, labels_ref.shape[1]), 0)
    block = jnp.where(row < CX, 2 * row, 2 * (row - CX) + 1)
    chosen = (block == labels_ref[...]).astype(jnp.bfloat16)
    dims = (((1,), (0,)), ((), ()))
    for level in range(NF):
        data = slots_ref[pl.ds(level, labels_ref.shape[1], stride=NF), :]
        high = data.astype(jnp.bfloat16)
        low = (data - high.astype(jnp.float32)).astype(jnp.bfloat16)
        total = lax.dot_general(chosen, high, dims, preferred_element_type=jnp.float32)
        total += lax.dot_general(chosen, low, dims, preferred_element_type=jnp.float32)
        total = jnp.concatenate([total[:CX], total[CX:]], axis=1)
        remapped_ref[level] = total
        surface = surface_ref[level]
        state_ref[level] = surface + coef_ref[...] * jnp.tanh(total - surface)


def body(
    air_sea_state, diffusion, courant, exchange_coef, src_block, dest_peer, dest_block, remap_weight
):
    peers = lax.axis_size("gx") * lax.axis_size("gy")
    slots = peers * CAP
    at_x, at_y = lax.axis_index("gx"), lax.axis_index("gy")
    x = air_sea_state[0]
    smem = pl.BlockSpec(memory_space=pltpu.SMEM)
    vmem = pl.BlockSpec(memory_space=pltpu.VMEM)
    limit = pltpu.CompilerParams(vmem_limit_bytes=48 << 20)

    meta = jnp.stack(
        [
            at_x * CX,
            at_y * CY,
            lax.axis_size("gx") * CX,
            lax.axis_size("gy") * CY,
            jnp.where(lax.axis_index("sec") == 0, STEPS_A, STEPS_O),
        ]
    ).astype(jnp.int32)
    rates = jnp.concatenate([diffusion, courant], axis=0)

    with jax.named_scope("routes"):
        target = dest_peer[0][:, 0]
        entry = jnp.arange(EPD, dtype=jnp.int32)
        earlier = (target[:, None] == target[None, :]) & (entry[None, :] < entry[:, None])
        position = target * CAP + jnp.sum(earlier.astype(jnp.int32), axis=1)
        route = jnp.stack([src_block[0], position])
        filled = position[None, :] == jnp.arange(slots, dtype=jnp.int32)[:, None]
        labels = jnp.sum(jnp.where(filled, dest_block[0][None, :] + 1, 0), axis=1) - 1
        labels = lax.all_gather(labels, ("gx", "gy"), axis=0, tiled=False)
        labels = lax.dynamic_slice_in_dim(labels, (at_x * lax.axis_size("gy") + at_y) * CAP, CAP, 1)
        labels = lax.ppermute(labels.reshape(1, slots), "sec", ring("sec", 1))

    with jax.named_scope("halo"):
        top = lax.ppermute(x[:, CX - HALO :], "gx", ring("gx", 1))
        bottom = lax.ppermute(x[:, :HALO], "gx", ring("gx", -1))
        side = jax.ShapeDtypeStruct((ROWS, BLK), jnp.float32)
        left, right = pl.pallas_call(pack_kernel, out_shape=(side, side), name="pack")(
            x, top, bottom
        )
        from_right = lax.ppermute(left, "gy", ring("gy", -1))
        from_left = lax.ppermute(right, "gy", ring("gy", 1))

    tile = pl.BlockSpec((NF, CX, CY), lambda i: (0, 0, 0))
    edge = pl.BlockSpec((NF, HALO, CY), lambda i: (0, 0, 0))
    whole = pl.BlockSpec((ROWS, BLK), lambda i: (0, 0))
    outgoing, surface = pl.pallas_call(
        surface_kernel,
        grid=(1,),
        in_specs=[smem, smem, smem, tile, edge, edge, whole, whole, pl.BlockSpec(memory_space=pl.ANY)],
        out_specs=[pl.BlockSpec((slots, NF, BLK), lambda i: (0, 0, 0)), tile],
        out_shape=(
            jax.ShapeDtypeStruct((slots, NF, BLK), jnp.float32),
            jax.ShapeDtypeStruct((NF, CX, CY), jnp.float32),
        ),
        scratch_shapes=[
            pltpu.VMEM((EPD, BLK, BLK), jnp.float32),
            pltpu.VMEM((BPD * 8, BLK), jnp.float32),
            pltpu.VMEM((ROWS, COLS), jnp.float32),
            pltpu.SemaphoreType.DMA((N_CHUNKS,)),
        ],
        compiler_params=limit,
        name="surface",
    )(meta, rates, route, x, top, bottom, from_left, from_right, remap_weight[0])

    tile_up = pl.BlockSpec((NF, CX, CY), lambda i: (i + 1, 0, 0))
    edge_up = pl.BlockSpec((NF, HALO, CY), lambda i: (i + 1, 0, 0))
    aloft = pl.pallas_call(
        aloft_kernel,
        grid=(LEV // NF - 1,),
        in_specs=[smem, smem, tile_up, edge_up, edge_up, whole, whole],
        out_specs=tile_up,
        out_shape=jax.ShapeDtypeStruct((LEV, CX, CY), jnp.float32),
        scratch_shapes=[pltpu.VMEM((ROWS, COLS), jnp.float32)],
        compiler_params=limit,
        name="aloft",
    )(meta, rates, x, top, bottom, from_left, from_right)

    incoming = lax.all_to_all(
        outgoing.reshape(peers, CAP, NF, BLK), ("gx", "gy"), split_axis=0, concat_axis=0, tiled=True
    )
    incoming = lax.ppermute(incoming, "sec", ring("sec", 1))

    new_state, remapped = pl.pallas_call(
        finish_kernel,
        grid=(1,),
        in_specs=[
            pl.BlockSpec((slots * NF, BLK), lambda i: (0, 0)),
            pl.BlockSpec((1, slots), lambda i: (0, 0)),
            tile,
            pl.BlockSpec((CX, CY), lambda i: (0, 0)),
            pl.BlockSpec(memory_space=pl.ANY),
        ],
        out_specs=[tile, tile],
        out_shape=(
            jax.ShapeDtypeStruct((LEV, CX, CY), jnp.float32),
            jax.ShapeDtypeStruct((NF, CX, CY), jnp.float32),
        ),
        input_output_aliases={4: 0},
        compiler_params=limit,
        name="finish",
    )(incoming.reshape(slots * NF, BLK), labels, surface, exchange_coef[0], aloft)
    return (new_state[None], remapped[None])


def solution(mesh):
    in_specs = (
        P("sec", None, "gx", "gy"),
        P("sec", None),
        P("sec", None),
        P("sec", "gx", "gy"),
        P("sec", ("gx", "gy")),
        P("sec", ("gx", "gy"), None),
        P("sec", ("gx", "gy")),
        P("sec", ("gx", "gy"), None, None),
    )
    out_specs = (P("sec", None, "gx", "gy"), P("sec", None, "gx", "gy"))
    return jax.shard_map(body, mesh=mesh, in_specs=in_specs, out_specs=out_specs, check_vma=False)
```

time: 245 us -> 426 us (1.74)
  blocking collectives: 63.6 us -> 284 us
  matrix products: 22.7 us -> 0 us
  Pallas kernels: 0 us -> 22 us
  waiting for transfers between devices: 37.5 us -> 23.2 us
  starting transfers between devices: 94.2 us -> 84.4 us
  other arithmetic: 12.5 us -> 3.13 us
  local copies, waits for them, and re-layouts: 12.8 us -> 5.23 us
    all_gather x0 -> x1, blocking collectives: none -> 284 us  [body(): labels = lax.all_gather(labels, ('gx', 'gy'), axis=0, tiled=False)]
    all_to_all x2 -> x0, blocking collectives: 63.6 us -> none  [the longest x1 47 us: remap_surface(): lax.all_to_all(outgoing.reshape(peer_count, capacity, levels_n, BLK), ('g...]
    ppermute x26 -> x6, waiting for transfers between devices: 37.5 us -> 3.45 us  [the longest x1 2.7 us: body(): top = lax.ppermute(x[:, CX - HALO:], 'gx', ring('gx', 1))]
    dot_general x2 -> x0, matrix products: 22.7 us -> none  [the longest x1 22.1 us: remap_surface(): jnp.einsum('eij,efj->efi', weights, picked, precision=lax.Precision.HIGHEST)]
    pallas_call x0 -> x4, Pallas kernels: none -> 22 us  [the longest x1 11.6 us: body(): pl.pallas_call(surface_kernel, grid=(1,), in_specs=[smem, smem, smem, til...]
    all_to_all x0 -> x1, waiting for transfers between devices: none -> 19.8 us  [body(): lax.all_to_all(outgoing.reshape(peers, CAP, NF, BLK), ('gx', 'gy'), split...]
    ppermute x26 -> x6, starting transfers between devices: 94.2 us -> 74.5 us  [the longest x1 55.8 us: body(): labels = lax.ppermute(labels.reshape(1, slots), 'sec', ring('sec', 1))]
    all_to_all x0 -> x1, starting transfers between devices: none -> 9.96 us  [body(): lax.all_to_all(outgoing.reshape(peers, CAP, NF, BLK), ('gx', 'gy'), split...]
  transfers between devices with their start and end apart: 26 -> 7, of which waited for: 19 -> 3; matrix products, arithmetic and copies ran while one was open for 1% -> 1% of each run, Pallas kernels for 0% -> 2%
where the time goes in v1:
time: 426 us; the launch traced here: 423 us
  blocking collectives  284 us (67%)
  starting transfers between devices  84.4 us (20%)
  waiting for transfers between devices  23.2 us (5%)
  Pallas kernels  22 us (5%)
  local copies, waits for them, and re-layouts  5.23 us (1%)
    all_gather x1, blocking collectives, body(): labels = lax.all_gather(labels, ('gx', 'gy'), axis=0, tiled=False)  284 us
    ppermute x1, starting transfers between devices, body(): labels = lax.ppermute(labels.reshape(1, slots), 'sec', ring('sec', 1))  55.8 us
    all_to_all x1, waiting for transfers between devices, body(): lax.all_to_all(outgoing.reshape(peers, CAP, NF, BLK), ('gx', 'gy'), split...  19.8 us
    pallas_call x1, Pallas kernels, body(): pl.pallas_call(surface_kernel, grid=(1,), in_specs=[smem, smem, smem, til...  11.6 us
    all_to_all x1, starting transfers between devices, body(): lax.all_to_all(outgoing.reshape(peers, CAP, NF, BLK), ('gx', 'gy'), split...  9.96 us
  transfers between devices with their start and end apart: 7, of which 3 were waited for; matrix products, arithmetic and copies ran while one was open for 1% of the time, Pallas kernels for 2%

profile of v1, /device:TPU:1, one launch (start us, length us, event | category | flops | bytes accessed | tf_op | source)
XLA Modules:
  0.0 422.9 jit_solution(7982275754934784974)
XLA Ops:
  0.6 0.0 copy-start.1
  0.6 0.0 copy-start.9
  0.7 1.1 fusion.1
  1.7 6.5 %collective-permute-start.1 = (f32[16,8,256]{2,1,0:T(8,128)S(1)}, f32[16,8,256]{2,1,0:T(8,128)S(1)}, u32[]{:S(2)}, u32[]{:S(2)}) collective-permute-start(f32[16,8,256]{2,1,0:T(8,128)S(1)} %get-tuple-element.14), channel_id=1, source_target_pairs={{0,112},{16,0},{32,16},{48,32},{64,48},{80,64},{96,80},{112,96},{1... | collective-permute-start | bytes 393224 | tf_op jit(solution)/shard_map/halo/ppermute | solution.py:188
  8.2 0.0 collective-permute-start
  8.2 0.9 convert_reduce_fusion
  9.2 0.7 bitcast_add_fusion
  9.8 0.7 pad_add_fusion.route_ref
  10.5 0.0 collective-permute-done.1.bottom_ref
  10.6 2.7 collective-permute-done.top_ref
  13.3 0.7 copy-done.5
  13.9 2.1 pack.1
  16.1 1.2 collective-permute-start.2
  17.3 3.7 collective-permute-start.3
  21.0 0.7 pad_maximum_fusion.rates_ref
  21.7 0.1 stack.19.meta_ref
  21.8 0.7 collective-permute-done.2.left_ref
  22.5 0.0 collective-permute-done.3.right_ref
  22.5 1.1 copy-done
  23.6 0.9 copy-done.3
  24.5 0.9 copy-done.6
  25.5 11.6 %surface.1 = (f32[384,4,128]{2,1,0:T(4,128)}, f32[4,48,256]{2,1,0:T(8,128)S(1)}) custom-call(s32[5]{0:T(128)S(1)} %stack.19.meta_ref, f32[2,16]{1,0:T(2,128)S(1)} %pad_maximum_fusion.rates_ref, s32[2,192]{1,0:T(2,128)S(1)} %pad_add_fusion.route_ref, f32[16,48,256]{2,1,0:T(8,128)S(1)} %bitcast.17, f32[16,8,256]{2,1,0:T(8,128)S(1)} %copy-done.6, ...), custom_call_target="tpu_custom_call" | custom-call | tf_op jit(solution)/shard_map/surface/pallas_call | solution.py:199
  37.0 10.0 %all-to-all-start = ((f32[128,3,4,128]{3,2,1,0:T(4,128)}), f32[128,3,4,128]{3,2,1,0:T(4,128)S(1)}, u32[]{:S(2)}, u32[]{:S(2)}) async-start(f32[128,3,4,128]{3,2,1,0:T(4,128)} %bitcast.8), calls=%async_computation | async-start | bytes 1572864 | tf_op jit(solution)/shard_map/all_to_all | solution.py:231
  47.0 19.8 %all-to-all-done = f32[128,3,4,128]{3,2,1,0:T(4,128)S(1)} async-done(((f32[128,3,4,128]{3,2,1,0:T(4,128)}), f32[128,3,4,128]{3,2,1,0:T(4,128)S(1)}, u32[]{:S(2)}, u32[]{:S(2)}) %all-to-all-start) | async-done | bytes 786464 | tf_op jit(solution)/shard_map/all_to_all | solution.py:231
  66.8 7.3 %collective-permute-start.4 = (f32[128,3,4,128]{3,2,1,0:T(4,128)S(1)}, f32[128,3,4,128]{3,2,1,0:T(4,128)S(1)}, u32[]{:S(2)}, u32[]{:S(2)}) collective-permute-start(f32[128,3,4,128]{3,2,1,0:T(4,128)S(1)} %all-to-all-done), channel_id=1, source_target_pairs={{0,128},{128,0},{1,129},{129,1},{2,130},{130,2},{3,131},{131,3},{4... | collective-permute-start | bytes 2359304 | tf_op jit(solution)/shard_map/ppermute | solution.py:234
  74.1 0.1 select_reduce_fusion
  74.2 284.2 %all-gather.1 = s32[128,1,384]{2,1,0:T(1,128)S(1)} all-gather(s32[1,1,384]{2,1,0:T(1,128)S(1)} %reshape.48), channel_id=2, replica_groups=mesh['sec'=2,'gx'=8,'gy'=16] {'gx','gy'}, dimensions={0}, use_global_device_ids=true | all-gather | bytes 198144 | tf_op jit(solution)/shard_map/routes/all_gather | solution.py:182
  358.4 0.2 dynamic-slice_reduce_fusion
  358.7 0.2 reshape.46
  358.9 55.8 %collective-permute-start.5 = (s32[1,384]{1,0:T(1,128)S(1)}, s32[1,384]{1,0:T(1,128)S(1)}, u32[]{:S(2)}, u32[]{:S(2)}) collective-permute-start(s32[1,384]{1,0:T(1,128)S(1)} %reshape.46), channel_id=1, source_target_pairs={{0,128},{128,0},{1,129},{129,1},{2,130},{130,2},{3,131},{131,3},{4... | collective-permute-start | bytes 4616 | tf_op jit(solution)/shard_map/routes/ppermute | solution.py:184
  414.6 7.1 %aloft.1.aloft_ref = f32[16,48,256]{2,1,0:T(8,128)} custom-call(s32[5]{0:T(128)S(1)} %stack.19.meta_ref, f32[2,16]{1,0:T(2,128)S(1)} %pad_maximum_fusion.rates_ref, f32[16,48,256]{2,1,0:T(8,128)S(1)} %bitcast.18, f32[16,8,256]{2,1,0:T(8,128)S(1)} %copy-done.7, f32[16,8,256]{2,1,0:T(8,128)S(1)} %copy-done.4, f32[64,128]{1,0:T(8,128)S(1)} %collective-permute-done.2.left_ref, ...), custom_call_target="tpu_custom_call" | custom-call | tf_op jit(solution)/shard_map/aloft/pallas_call | solution.py:220
  421.8 1.1 finish.1
  (22 shorter events, 0.1 us)
Async XLA Ops:
  0.6 414.0 %copy-start.1 = (f32[1,16,48,256]{3,2,1,0:T(8,128)S(1)}, f32[1,16,48,256]{3,2,1,0:T(8,128)}, u32[]{:S(2)}) copy-start(f32[1,16,48,256]{3,2,1,0:T(8,128)} %param.8) | copy-start | bytes 2359300
  0.6 73.4 %copy-start.9 = (s32[1,192,1]{1,2,0:T(1,128)S(1)}, s32[1,192,1]{1,2,0:T(1,128)}, u32[]{:S(2)}) copy-start(s32[1,192,1]{1,2,0:T(1,128)} %param.13) | copy-start | bytes 2308
  0.7 73.4 %copy-start.10 = (s32[1,192]{1,0:T(1,128)S(1)}, s32[1,192]{1,0:T(1,128)}, u32[]{:S(2)}) copy-start(s32[1,192]{1,0:T(1,128)} %param.14) | copy-start | bytes 2308
  0.7 421.1 %copy-start.8 = (f32[1,48,256]{2,1,0:T(8,128)S(1)}, f32[1,48,256]{2,1,0:T(8,128)}, u32[]{:S(2)}) copy-start(f32[1,48,256]{2,1,0:T(8,128)} %param.11) | copy-start | bytes 147460
  1.7 8.8 %collective-permute-start.1 = (f32[16,8,256]{2,1,0:T(8,128)S(1)}, f32[16,8,256]{2,1,0:T(8,128)S(1)}, u32[]{:S(2)}, u32[]{:S(2)}) collective-permute-start(f32[16,8,256]{2,1,0:T(8,128)S(1)} %get-tuple-element.14), channel_id=1, source_target_pairs={{0,112},{16,0},{32,16},{48,32},{64,48},{80,64},{96,80},{112,96},{1... | collective-permute-start | bytes 393224 | tf_op jit(solution)/shard_map/halo/ppermute | solution.py:188
  8.2 5.0 %collective-permute-start = (f32[16,8,256]{2,1,0:T(8,128)S(1)}, f32[16,8,256]{2,1,0:T(8,128)S(1)}, u32[]{:S(2)}, u32[]{:S(2)}) collective-permute-start(f32[16,8,256]{2,1,0:T(8,128)S(1)} %get-tuple-element.15), channel_id=1, source_target_pairs={{0,16},{16,32},{32,48},{48,64},{64,80},{80,96},{96,112},{112,0},{1... | collective-permute-start | bytes 393224 | tf_op jit(solution)/shard_map/halo/ppermute | solution.py:187
  10.5 2.7 copy-start.2
  13.3 0.7 copy-start.5
  16.1 6.4 %collective-permute-start.2 = (f32[64,128]{1,0:T(8,128)}, f32[64,128]{1,0:T(8,128)S(1)}, u32[]{:S(2)}, u32[]{:S(2)}) collective-permute-start(f32[64,128]{1,0:T(8,128)} %get-tuple-element.8), channel_id=1, source_target_pairs={{0,1},{1,2},{2,3},{3,4},{4,5},{5,6},{6,7},{7,8},{8,9},{9,10},{10,1... | collective-permute-start | bytes 98312 | tf_op jit(solution)/shard_map/halo/ppermute | solution.py:194
  17.3 5.2 %collective-permute-start.3 = (f32[64,128]{1,0:T(8,128)}, f32[64,128]{1,0:T(8,128)S(1)}, u32[]{:S(2)}, u32[]{:S(2)}) collective-permute-start(f32[64,128]{1,0:T(8,128)} %get-tuple-element.9), channel_id=1, source_target_pairs={{0,15},{1,0},{2,1},{3,2},{4,3},{5,4},{6,5},{7,6},{8,7},{9,8},{10,9... | collective-permute-start | bytes 98312 | tf_op jit(solution)/shard_map/halo/ppermute | solution.py:193
  22.5 1.1 copy-start
  23.6 0.9 copy-start.3
  24.5 0.9 copy-start.6
  25.4 389.2 %copy-start.4 = (f32[16,8,256]{2,1,0:T(8,128)S(1)}, f32[16,8,256]{2,1,0:T(8,128)}, u32[]{:S(2)}) copy-start(f32[16,8,256]{2,1,0:T(8,128)} %copy-done.2) | copy-start | bytes 393220
  25.5 389.2 %copy-start.7 = (f32[16,8,256]{2,1,0:T(8,128)S(1)}, f32[16,8,256]{2,1,0:T(8,128)}, u32[]{:S(2)}) copy-start(f32[16,8,256]{2,1,0:T(8,128)} %copy-done.5) | copy-start | bytes 393220
  37.0 29.7 %all-to-all-start = ((f32[128,3,4,128]{3,2,1,0:T(4,128)}), f32[128,3,4,128]{3,2,1,0:T(4,128)S(1)}, u32[]{:S(2)}, u32[]{:S(2)}) async-start(f32[128,3,4,128]{3,2,1,0:T(4,128)} %bitcast.8), calls=%async_computation | async-start | bytes 1572864 | tf_op jit(solution)/shard_map/all_to_all | solution.py:231
  66.8 355.0 %collective-permute-start.4 = (f32[128,3,4,128]{3,2,1,0:T(4,128)S(1)}, f32[128,3,4,128]{3,2,1,0:T(4,128)S(1)}, u32[]{:S(2)}, u32[]{:S(2)}) collective-permute-start(f32[128,3,4,128]{3,2,1,0:T(4,128)S(1)} %all-to-all-done), channel_id=1, source_target_pairs={{0,128},{128,0},{1,129},{129,1},{2,130},{130,2},{3,131},{131,3},{4... | collective-permute-start | bytes 2359304 | tf_op jit(solution)/shard_map/ppermute | solution.py:234
  358.9 62.9 %collective-permute-start.5 = (s32[1,384]{1,0:T(1,128)S(1)}, s32[1,384]{1,0:T(1,128)S(1)}, u32[]{:S(2)}, u32[]{:S(2)}) collective-permute-start(s32[1,384]{1,0:T(1,128)S(1)} %reshape.46), channel_id=1, source_target_pairs={{0,128},{128,0},{1,129},{129,1},{2,130},{130,2},{3,131},{131,3},{4... | collective-permute-start | bytes 4616 | tf_op jit(solution)/shard_map/routes/ppermute | solution.py:184

commit v2 on v1

--- a/solution.py
+++ b/solution.py
@@ -20,6 +20,7 @@
 COLS = CY + BLK
 CHUNK = 16
 N_CHUNKS = EPD // CHUNK
+ROWS_PER_PEER = CAP * NF + 1
 
 
 def ring(axis, shift):
@@ -70,17 +71,21 @@
     right_ref[...] = right
 
 
+def split_kernel(w_ref, *refs):
+    high_ref, low_ref = refs[-2:]
+    rows = pl.ds(pl.program_id(0) * CHUNK, CHUNK)
+    weight = w_ref[...]
+    high = weight.astype(jnp.bfloat16)
+    high_ref[rows] = high
+    low_ref[rows] = (weight - high.astype(jnp.float32)).astype(jnp.bfloat16)
+
+
 def surface_kernel(
-    meta_ref, rates_ref, route_ref, x_ref, top_ref, bottom_ref, left_ref, right_ref, w_ref,
-    slots_ref, surface_ref, w_buf, blocks, keep_ref, sems,
+    meta_ref, rates_ref, route_ref, x_ref, top_ref, bottom_ref, left_ref, right_ref, label_ref,
+    high_ref, low_ref, slots_ref, surface_ref, blocks, keep_ref,
 ):
-    def fetch(part):
-        rows = pl.ds(part * CHUNK, CHUNK)
-        return pltpu.make_async_copy(w_ref.at[rows], w_buf.at[rows], sems.at[part])
-
-    for part in range(N_CHUNKS):
-        fetch(part).start()
     slots_ref[...] = jnp.zeros(slots_ref.shape, jnp.float32)
+    slots_ref[pl.ds(ROWS_PER_PEER - 1, label_ref.shape[0], stride=ROWS_PER_PEER), :] = label_ref[...]
     keep_ref[...] = inside(meta_ref).astype(jnp.float32)
     for level in range(NF):
         field = extended(
@@ -98,17 +103,13 @@
 
     def entry(e):
         picked = blocks[pl.ds(pl.multiple_of(route_ref[0, e] * 8, 8), 8), :].astype(jnp.bfloat16)
-        weight = w_buf[e]
-        high = weight.astype(jnp.bfloat16)
-        low = (weight - high.astype(jnp.float32)).astype(jnp.bfloat16)
         dims = (((1,), (1,)), ((), ()))
-        both = lax.dot_general(picked, high, dims, preferred_element_type=jnp.float32)
-        both += lax.dot_general(picked, low, dims, preferred_element_type=jnp.float32)
-        slots_ref[route_ref[1, e]] = both[:NF] + both[NF:]
+        both = lax.dot_general(picked, high_ref[e], dims, preferred_element_type=jnp.float32)
+        both += lax.dot_general(picked, low_ref[e], dims, preferred_element_type=jnp.float32)
+        slots_ref[pl.ds(route_ref[1, e], NF), :] = both[:NF] + both[NF:]
 
     @pl.loop(0, N_CHUNKS)
     def _(part):
-        fetch(part).wait()
         for k in range(CHUNK):
             entry(part * CHUNK + k)
 
@@ -131,18 +132,22 @@
         out_ref[k] = field[:CX, :CY]
 
 
-def finish_kernel(slots_ref, labels_ref, surface_ref, coef_ref, aloft_ref, state_ref, remapped_ref):
+def finish_kernel(slots_ref, surface_ref, coef_ref, aloft_ref, state_ref, remapped_ref):
     del aloft_ref
-    row = lax.broadcasted_iota(jnp.int32, (BPD, labels_ref.shape[1]), 0)
-    block = jnp.where(row < CX, 2 * row, 2 * (row - CX) + 1)
-    chosen = (block == labels_ref[...]).astype(jnp.bfloat16)
+    peers = slots_ref.shape[0] // ROWS_PER_PEER
+    labels = slots_ref[pl.ds(ROWS_PER_PEER - 1, peers, stride=ROWS_PER_PEER), :].T
+    row = lax.broadcasted_iota(jnp.int32, (BPD, peers), 0)
+    block = jnp.where(row < CX, 2 * row, 2 * (row - CX) + 1).astype(jnp.float32)
+    chosen = [(block == labels[k : k + 1]).astype(jnp.bfloat16) for k in range(CAP)]
     dims = (((1,), (0,)), ((), ()))
     for level in range(NF):
-        data = slots_ref[pl.ds(level, labels_ref.shape[1], stride=NF), :]
-        high = data.astype(jnp.bfloat16)
-        low = (data - high.astype(jnp.float32)).astype(jnp.bfloat16)
-        total = lax.dot_general(chosen, high, dims, preferred_element_type=jnp.float32)
-        total += lax.dot_general(chosen, low, dims, preferred_element_type=jnp.float32)
+        total = jnp.zeros((BPD, BLK), jnp.float32)
+        for k in range(CAP):
+            data = slots_ref[pl.ds(k * NF + level, peers, stride=ROWS_PER_PEER), :]
+            high = data.astype(jnp.bfloat16)
+            low = (data - high.astype(jnp.float32)).astype(jnp.bfloat16)
+            total += lax.dot_general(chosen[k], high, dims, preferred_element_type=jnp.float32)
+            total += lax.dot_general(chosen[k], low, dims, preferred_element_type=jnp.float32)
         total = jnp.concatenate([total[:CX], total[CX:]], axis=1)
         remapped_ref[level] = total
         surface = surface_ref[level]
@@ -153,12 +158,14 @@
     air_sea_state, diffusion, courant, exchange_coef, src_block, dest_peer, dest_block, remap_weight
 ):
     peers = lax.axis_size("gx") * lax.axis_size("gy")
-    slots = peers * CAP
+    rows_out = peers * ROWS_PER_PEER
     at_x, at_y = lax.axis_index("gx"), lax.axis_index("gy")
     x = air_sea_state[0]
     smem = pl.BlockSpec(memory_space=pltpu.SMEM)
     vmem = pl.BlockSpec(memory_space=pltpu.VMEM)
-    limit = pltpu.CompilerParams(vmem_limit_bytes=48 << 20)
+
+    def limit(mib):
+        return pltpu.CompilerParams(vmem_limit_bytes=mib << 20)
 
     meta = jnp.stack(
         [
@@ -175,21 +182,38 @@
         target = dest_peer[0][:, 0]
         entry = jnp.arange(EPD, dtype=jnp.int32)
         earlier = (target[:, None] == target[None, :]) & (entry[None, :] < entry[:, None])
-        position = target * CAP + jnp.sum(earlier.astype(jnp.int32), axis=1)
-        route = jnp.stack([src_block[0], position])
-        filled = position[None, :] == jnp.arange(slots, dtype=jnp.int32)[:, None]
-        labels = jnp.sum(jnp.where(filled, dest_block[0][None, :] + 1, 0), axis=1) - 1
-        labels = lax.all_gather(labels, ("gx", "gy"), axis=0, tiled=False)
-        labels = lax.dynamic_slice_in_dim(labels, (at_x * lax.axis_size("gy") + at_y) * CAP, CAP, 1)
-        labels = lax.ppermute(labels.reshape(1, slots), "sec", ring("sec", 1))
+        rank = jnp.sum(earlier.astype(jnp.int32), axis=1)
+        route = jnp.stack([src_block[0], target * ROWS_PER_PEER + rank * NF])
+        to_peer = target[None, :] == jnp.arange(peers, dtype=jnp.int32)[:, None]
+        label = [
+            jnp.sum(jnp.where(to_peer & (rank == k)[None, :], dest_block[0][None, :] + 1, 0), axis=1)
+            for k in range(CAP)
+        ]
+        label = jnp.stack(label, axis=1).astype(jnp.float32) - 1.0
+        label = jnp.pad(label, ((0, 0), (0, BLK - CAP)), constant_values=-1.0)
+
+    with jax.named_scope("split"):
+        part = pl.BlockSpec((CHUNK, BLK, BLK), lambda i: (i, 0, 0))
+        half = pltpu.VMEM((EPD, BLK, BLK), jnp.bfloat16)
+        high, low = pl.pallas_call(
+            split_kernel,
+            grid=(N_CHUNKS,),
+            in_specs=[part] + [pl.BlockSpec(memory_space=pl.ANY)] * 4,
+            out_specs=[vmem, vmem],
+            out_shape=(half, half),
+            compiler_params=limit(6),
+            name="split",
+        )(
+            pltpu.with_memory_space_constraint(remap_weight[0], pltpu.HBM), meta, rates, route, label
+        )
 
     with jax.named_scope("halo"):
         top = lax.ppermute(x[:, CX - HALO :], "gx", ring("gx", 1))
         bottom = lax.ppermute(x[:, :HALO], "gx", ring("gx", -1))
         side = jax.ShapeDtypeStruct((ROWS, BLK), jnp.float32)
-        left, right = pl.pallas_call(pack_kernel, out_shape=(side, side), name="pack")(
-            x, top, bottom
-        )
+        left, right = pl.pallas_call(
+            pack_kernel, out_shape=(side, side), compiler_params=limit(3), name="pack"
+        )(x, top, bottom)
         from_right = lax.ppermute(left, "gy", ring("gy", -1))
         from_left = lax.ppermute(right, "gy", ring("gy", 1))
 
@@ -199,21 +223,22 @@
     outgoing, surface = pl.pallas_call(
         surface_kernel,
         grid=(1,),
-        in_specs=[smem, smem, smem, tile, edge, edge, whole, whole, pl.BlockSpec(memory_space=pl.ANY)],
-        out_specs=[pl.BlockSpec((slots, NF, BLK), lambda i: (0, 0, 0)), tile],
+        in_specs=[
+            smem, smem, smem, tile, edge, edge, whole, whole,
+            pl.BlockSpec((peers, BLK), lambda i: (0, 0)), vmem, vmem,
+        ],
+        out_specs=[pl.BlockSpec((rows_out, BLK), lambda i: (0, 0)), tile],
         out_shape=(
-            jax.ShapeDtypeStruct((slots, NF, BLK), jnp.float32),
+            jax.ShapeDtypeStruct((rows_out, BLK), jnp.float32),
             jax.ShapeDtypeStruct((NF, CX, CY), jnp.float32),
         ),
         scratch_shapes=[
-            pltpu.VMEM((EPD, BLK, BLK), jnp.float32),
             pltpu.VMEM((BPD * 8, BLK), jnp.float32),
             pltpu.VMEM((ROWS, COLS), jnp.float32),
-            pltpu.SemaphoreType.DMA((N_CHUNKS,)),
         ],
-        compiler_params=limit,
+        compiler_params=limit(6),
         name="surface",
-    )(meta, rates, route, x, top, bottom, from_left, from_right, remap_weight[0])
+    )(meta, rates, route, x, top, bottom, from_left, from_right, label, high, low)
 
     tile_up = pl.BlockSpec((NF, CX, CY), lambda i: (i + 1, 0, 0))
     edge_up = pl.BlockSpec((NF, HALO, CY), lambda i: (i + 1, 0, 0))
@@ -224,21 +249,20 @@
         out_specs=tile_up,
         out_shape=jax.ShapeDtypeStruct((LEV, CX, CY), jnp.float32),
         scratch_shapes=[pltpu.VMEM((ROWS, COLS), jnp.float32)],
-        compiler_params=limit,
+        compiler_params=limit(4),
         name="aloft",
     )(meta, rates, x, top, bottom, from_left, from_right)
 
     incoming = lax.all_to_all(
-        outgoing.reshape(peers, CAP, NF, BLK), ("gx", "gy"), split_axis=0, concat_axis=0, tiled=True
+        outgoing.reshape(peers, ROWS_PER_PEER, 1, BLK), ("gx", "gy"), split_axis=0, concat_axis=0, tiled=True
     )
-    incoming = lax.ppermute(incoming, "sec", ring("sec", 1))
+    incoming = lax.ppermute(incoming.reshape(rows_out, BLK), "sec", ring("sec", 1))
 
     new_state, remapped = pl.pallas_call(
         finish_kernel,
         grid=(1,),
         in_specs=[
-            pl.BlockSpec((slots * NF, BLK), lambda i: (0, 0)),
-            pl.BlockSpec((1, slots), lambda i: (0, 0)),
+            pl.BlockSpec((rows_out, BLK), lambda i: (0, 0)),
             tile,
             pl.BlockSpec((CX, CY), lambda i: (0, 0)),
             pl.BlockSpec(memory_space=pl.ANY),
@@ -248,10 +272,10 @@
             jax.ShapeDtypeStruct((LEV, CX, CY), jnp.float32),
             jax.ShapeDtypeStruct((NF, CX, CY), jnp.float32),
         ),
-        input_output_aliases={4: 0},
-        compiler_params=limit,
+        input_output_aliases={3: 0},
+        compiler_params=limit(5),
         name="finish",
-    )(incoming.reshape(slots * NF, BLK), labels, surface, exchange_coef[0], aloft)
+    )(incoming, surface, exchange_coef[0], aloft)
     return (new_state[None], remapped[None])
 
 

time: 426 us -> 87.2 us (0.20)
  the two profiles are of different devices: /device:TPU:1 before, /device:TPU:8 now
where the time goes in v2:
time: 87.2 us; the launch traced here: 86.8 us
  blocking collectives  34.6 us (40%)
  Pallas kernels  34.3 us (39%)
  starting transfers between devices  10.2 us (12%)
  other arithmetic  4.58 us (5%)
  local copies, waits for them, and re-layouts  2.33 us (3%)
    all_to_all x1, blocking collectives, body(): lax.all_to_all(outgoing.reshape(peers, ROWS_PER_PEER, 1, BLK), ('gx', 'gy...  34.6 us
    pallas_call x1, Pallas kernels, body(): pl.pallas_call(surface_kernel, grid=(1,), in_specs=[smem, smem, smem, til...  12 us
    pallas_call x1, Pallas kernels, body(): pl.pallas_call(aloft_kernel, grid=(LEV // NF - 1,), in_specs=[smem, smem,...  11.8 us
    pallas_call x1, Pallas kernels, body(): pl.pallas_call(split_kernel, grid=(N_CHUNKS,), in_specs=[part] + [pl.Bloc...  8.95 us
    ppermute x1, starting transfers between devices, body(): bottom = lax.ppermute(x[:, :HALO], 'gx', ring('gx', -1))  4.03 us
    ppermute x1, starting transfers between devices, body(): from_right = lax.ppermute(left, 'gy', ring('gy', -1))  2.64 us
    ppermute x1, starting transfers between devices, body(): top = lax.ppermute(x[:, CX - HALO:], 'gx', ring('gx', 1))  1.99 us
  transfers between devices with their start and end apart: 5, of which 0 were waited for; matrix products, arithmetic and copies ran while one was open for 6% of the time, Pallas kernels for 24%

profile of v2, /device:TPU:8, one launch (start us, length us, event | category | flops | bytes accessed | tf_op | source)
XLA Modules:
  0.0 86.8 jit_solution(3976993550897587528)
XLA Ops:
  0.6 1.0 %fusion.4 = (f32[16,8,256]{2,1,0:T(8,128)S(1)}, f32[16,8,256]{2,1,0:T(8,128)S(1)}) fusion(f32[16,48,256]{2,1,0:T(8,128)} %bitcast.18), kind=kLoop, calls=%fused_computation.20 | loop fusion | bytes 524288 | tf_op jit(solution)/shard_map/halo/slice | solution.py:212
  1.6 2.0 %collective-permute-start = (f32[16,8,256]{2,1,0:T(8,128)S(1)}, f32[16,8,256]{2,1,0:T(8,128)S(1)}, u32[]{:S(2)}, u32[]{:S(2)}) collective-permute-start(f32[16,8,256]{2,1,0:T(8,128)S(1)} %get-tuple-element.22), channel_id=1, source_target_pairs={{0,16},{16,32},{32,48},{48,64},{64,80},{80,96},{96,112},{112,0},{1... | collective-permute-start | bytes 393224 | tf_op jit(solution)/shard_map/halo/ppermute | solution.py:211
  3.6 4.0 %collective-permute-start.1 = (f32[16,8,256]{2,1,0:T(8,128)S(1)}, f32[16,8,256]{2,1,0:T(8,128)S(1)}, u32[]{:S(2)}, u32[]{:S(2)}) collective-permute-start(f32[16,8,256]{2,1,0:T(8,128)S(1)} %get-tuple-element.21), channel_id=1, source_target_pairs={{0,112},{16,0},{32,16},{48,32},{64,48},{80,64},{96,80},{112,96},{1... | collective-permute-start | bytes 393224 | tf_op jit(solution)/shard_map/halo/ppermute | solution.py:212
  7.6 0.9 %convert_reduce_fusion = s32[192]{0:T(256)S(1)} fusion(s32[192]{0:T(256)} %bitcast.27), kind=kLoop, calls=%fused_computation | loop fusion | flops 184128 | bytes 1536 | tf_op jit(solution)/shard_map/routes/reduce_sum | solution.py:185
  8.6 0.7 broadcast_add_fusion.1
  9.3 0.9 %select_reduce_fusion.2 = (s32[128]{0:T(128)S(1)}, s32[128]{0:T(128)S(1)}, s32[128]{0:T(128)S(1)}) fusion(s32[192]{0:T(256)S(1)} %bitcast.30, s32[192]{0:T(256)} %bitcast.28, pred[192]{0:T(512)(128)(4,1)S(1)} %get-tuple-element.25, pred[192]{0:T(512)(128)(4,1)S(1)} %get-tuple-element.24, pred[192]{0:T(512)(128)(4,1)S(1)} %get-tuple-element.23), kind=kLoop, calls=%fused_computation.5 | loop fusion | flops 245376 | bytes 3648 | tf_op jit(solution)/shard_map/routes/reduce_sum | solution.py:189
  10.2 0.1 copy.21
  10.3 0.7 bitcast_add_fusion
  11.0 0.7 pad_add_fusion.refs_2_.route_ref
  11.7 0.0 collective-permute-done.top_ref
  11.7 0.0 collective-permute-done.1.bottom_ref
  11.7 0.0 copy-start
  11.7 1.1 %copy-done = f32[1,16,48,256]{3,2,1,0:T(8,128)S(1)} copy-done((f32[1,16,48,256]{3,2,1,0:T(8,128)S(1)}, f32[1,16,48,256]{3,2,1,0:T(8,128)}, u32[]{:S(2)}) %copy-start) | copy-done | bytes 786456
  12.8 0.3 pack.1
  13.2 1.6 %collective-permute-start.2 = (f32[64,128]{1,0:T(8,128)S(1)}, f32[64,128]{1,0:T(8,128)S(1)}, u32[]{:S(2)}, u32[]{:S(2)}) collective-permute-start(f32[64,128]{1,0:T(8,128)S(1)} %get-tuple-element.10), channel_id=1, source_target_pairs={{0,1},{1,2},{2,3},{3,4},{4,5},{5,6},{6,7},{7,8},{8,9},{9,10},{10,1... | collective-permute-start | bytes 98312 | tf_op jit(solution)/shard_map/halo/ppermute | solution.py:218
  14.7 2.6 %collective-permute-start.3 = (f32[64,128]{1,0:T(8,128)S(1)}, f32[64,128]{1,0:T(8,128)S(1)}, u32[]{:S(2)}, u32[]{:S(2)}) collective-permute-start(f32[64,128]{1,0:T(8,128)S(1)} %get-tuple-element.11), channel_id=1, source_target_pairs={{0,15},{1,0},{2,1},{3,2},{4,3},{5,4},{6,5},{7,6},{8,7},{9,8},{10,9... | collective-permute-start | bytes 98312 | tf_op jit(solution)/shard_map/halo/ppermute | solution.py:217
  17.4 0.7 pad_maximum_fusion.refs_1_.rates_ref
  18.1 0.1 stack.31.refs_0_.meta_ref
  18.2 0.0 copy-start.1
  18.2 9.0 %split.1 = (bf16[192,128,128]{2,1,0:T(8,128)(2,1)S(1)}, bf16[192,128,128]{2,1,0:T(8,128)(2,1)S(1)}) custom-call(f32[192,128,128]{2,1,0:T(8,128)} %bitcast.24, s32[5]{0:T(128)S(1)} %stack.31.refs_0_.meta_ref, f32[2,16]{1,0:T(2,128)S(1)} %pad_maximum_fusion.refs_1_.rates_ref, s32[2,192]{1,0:T(2,128)S(1)} %pad_add_fusion.refs_2_.route_ref, ...), custom_call_target="tpu_custom_call" | custom-call | tf_op jit(solution)/shard_map/split/split/pallas_call | solution.py:198
  27.1 0.0 collective-permute-done.2.left_ref
  27.1 0.0 collective-permute-done.3.right_ref
  27.2 0.0 copy-done.1
  27.2 0.0 copy-start.2
  27.2 12.0 %surface.1 = (f32[1664,128]{1,0:T(8,128)S(1)}, f32[4,48,256]{2,1,0:T(8,128)S(1)}) custom-call(s32[5]{0:T(128)S(1)} %stack.31.refs_0_.meta_ref, f32[2,16]{1,0:T(2,128)S(1)} %pad_maximum_fusion.refs_1_.rates_ref, s32[2,192]{1,0:T(2,128)S(1)} %pad_add_fusion.refs_2_.route_ref, f32[16,48,256]{2,1,0:T(8,128)S(1)} %bitcast.20, ...), custom_call_target="tpu_custom_call" | custom-call | tf_op jit(solution)/shard_map/surface/pallas_call | solution.py:223
  39.2 34.6 %all_to_all.5 = f32[128,13,1,128]{3,2,1,0:T(1,128)S(1)} all-to-all(f32[128,13,1,128]{3,2,1,0:T(1,128)S(1)} %bitcast.22), channel_id=1, replica_groups=mesh['sec'=2,'gx'=8,'gy'=16] {'gx','gy'}, dimensions={0} | all-to-all | bytes 1703936 | tf_op jit(solution)/shard_map/all_to_all | solution.py:256
  73.8 0.0 collective-permute-start.4
  73.8 11.8 %aloft.1.aloft_ref = f32[16,48,256]{2,1,0:T(8,128)} custom-call(s32[5]{0:T(128)S(1)} %stack.31.refs_0_.meta_ref, f32[2,16]{1,0:T(2,128)S(1)} %pad_maximum_fusion.refs_1_.rates_ref, f32[16,48,256]{2,1,0:T(8,128)S(1)} %bitcast.21, f32[16,8,256]{2,1,0:T(8,128)S(1)} %collective-permute-done.top_ref, f32[16,8,256]{2,1,0:T(8,128)S(1)} %collective-permute-done.1.bottom_ref, ...), custom_call_target="tpu_custom_call" | custom-call | tf_op jit(solution)/shard_map/aloft/pallas_call | solution.py:245
  85.6 0.0 collective-permute-done.4.slots_ref
  85.6 0.0 copy-done.2
  85.6 1.2 %finish.1 = (f32[16,48,256]{2,1,0:T(8,128)}, f32[4,48,256]{2,1,0:T(8,128)}) custom-call(f32[1664,128]{1,0:T(8,128)S(1)} %collective-permute-done.4.slots_ref, f32[4,48,256]{2,1,0:T(8,128)S(1)} %get-tuple-element.15.surface_ref, f32[48,256]{1,0:T(8,128)S(1)} %bitcast.23, f32[16,48,256]{2,1,0:T(8,128)} %aloft.1.aloft_ref), custom_call_target="tpu_custom_call", output_to_operand_aliasing={{0}: (3, {})} | custom-call | tf_op jit(solution)/shard_map/finish/pallas_call | solution.py:261
  (5 shorter events, 0.0 us)
Async XLA Ops:
  1.6 10.1 %collective-permute-start = (f32[16,8,256]{2,1,0:T(8,128)S(1)}, f32[16,8,256]{2,1,0:T(8,128)S(1)}, u32[]{:S(2)}, u32[]{:S(2)}) collective-permute-start(f32[16,8,256]{2,1,0:T(8,128)S(1)} %get-tuple-element.22), channel_id=1, source_target_pairs={{0,16},{16,32},{32,48},{48,64},{64,80},{80,96},{96,112},{112,0},{1... | collective-permute-start | bytes 393224 | tf_op jit(solution)/shard_map/halo/ppermute | solution.py:211
  3.6 8.1 %collective-permute-start.1 = (f32[16,8,256]{2,1,0:T(8,128)S(1)}, f32[16,8,256]{2,1,0:T(8,128)S(1)}, u32[]{:S(2)}, u32[]{:S(2)}) collective-permute-start(f32[16,8,256]{2,1,0:T(8,128)S(1)} %get-tuple-element.21), channel_id=1, source_target_pairs={{0,112},{16,0},{32,16},{48,32},{64,48},{80,64},{96,80},{112,96},{1... | collective-permute-start | bytes 393224 | tf_op jit(solution)/shard_map/halo/ppermute | solution.py:212
  11.7 1.1 %copy-start = (f32[1,16,48,256]{3,2,1,0:T(8,128)S(1)}, f32[1,16,48,256]{3,2,1,0:T(8,128)}, u32[]{:S(2)}) copy-start(f32[1,16,48,256]{3,2,1,0:T(8,128)} %param.8) | copy-start | bytes 2359300
  13.2 14.0 %collective-permute-start.2 = (f32[64,128]{1,0:T(8,128)S(1)}, f32[64,128]{1,0:T(8,128)S(1)}, u32[]{:S(2)}, u32[]{:S(2)}) collective-permute-start(f32[64,128]{1,0:T(8,128)S(1)} %get-tuple-element.10), channel_id=1, source_target_pairs={{0,1},{1,2},{2,3},{3,4},{4,5},{5,6},{6,7},{7,8},{8,9},{9,10},{10,1... | collective-permute-start | bytes 98312 | tf_op jit(solution)/shard_map/halo/ppermute | solution.py:218
  14.7 12.4 %collective-permute-start.3 = (f32[64,128]{1,0:T(8,128)S(1)}, f32[64,128]{1,0:T(8,128)S(1)}, u32[]{:S(2)}, u32[]{:S(2)}) collective-permute-start(f32[64,128]{1,0:T(8,128)S(1)} %get-tuple-element.11), channel_id=1, source_target_pairs={{0,15},{1,0},{2,1},{3,2},{4,3},{5,4},{6,5},{7,6},{8,7},{9,8},{10,9... | collective-permute-start | bytes 98312 | tf_op jit(solution)/shard_map/halo/ppermute | solution.py:217
  18.2 9.0 %copy-start.1 = (f32[1,16,48,256]{3,2,1,0:T(8,128)S(1)}, f32[1,16,48,256]{3,2,1,0:T(8,128)}, u32[]{:S(2)}) copy-start(f32[1,16,48,256]{3,2,1,0:T(8,128)} %param.8) | copy-start | bytes 2359300
  27.2 58.4 %copy-start.2 = (f32[1,48,256]{2,1,0:T(8,128)S(1)}, f32[1,48,256]{2,1,0:T(8,128)}, u32[]{:S(2)}) copy-start(f32[1,48,256]{2,1,0:T(8,128)} %param.11) | copy-start | bytes 147460
  73.8 11.8 %collective-permute-start.4 = (f32[1664,128]{1,0:T(8,128)S(1)}, f32[1664,128]{1,0:T(8,128)S(1)}, u32[]{:S(2)}, u32[]{:S(2)}) collective-permute-start(f32[1664,128]{1,0:T(8,128)S(1)} %bitcast.26), channel_id=1, source_target_pairs={{0,128},{128,0},{1,129},{129,1},{2,130},{130,2},{3,131},{131,3},{4... | collective-permute-start | bytes 2555912 | tf_op jit(solution)/shard_map/ppermute | solution.py:259

commit v3 on v2

--- a/solution.py
+++ b/solution.py
@@ -21,6 +21,7 @@
 CHUNK = 16
 N_CHUNKS = EPD // CHUNK
 ROWS_PER_PEER = CAP * NF + 1
+UNROLL = 8
 
 
 def ring(axis, shift):
@@ -57,32 +58,84 @@
     return lax.fori_loop(0, steps, step, field)
 
 
-def pack_kernel(x_ref, top_ref, bottom_ref, left_ref, right_ref):
-    lane = lax.broadcasted_iota(jnp.int32, (ROWS, BLK), 1) // HALO
-    left = jnp.zeros((ROWS, BLK), jnp.float32)
-    right = jnp.zeros((ROWS, BLK), jnp.float32)
+def prepare_kernel(
+    w_ref, x_ref, source_ref, peer_ref, block_ref, meta_ref,
+    halves_ref, route_ref, label_ref, left_ref, right_ref, w_buf, x_buf, w_sems, x_sem,
+):
+    def fetch(part):
+        rows = pl.ds(part * CHUNK, CHUNK)
+        return pltpu.make_async_copy(w_ref.at[rows], w_buf.at[rows], w_sems.at[part])
+
+    tile = pltpu.make_async_copy(x_ref, x_buf, x_sem)
+    for part in range(2):
+        fetch(part).start()
+    tile.start()
+    for part in range(2, N_CHUNKS):
+        fetch(part).start()
+
+    target = peer_ref[...]
+    same = jnp.broadcast_to(target.astype(jnp.float32), (EPD, EPD))
+    same = same == same.T
+    first = lax.broadcasted_iota(jnp.int32, (EPD, EPD), 0)
+    second = lax.broadcasted_iota(jnp.int32, (EPD, EPD), 1)
+    rank = jnp.sum((same & (first < second)).astype(jnp.int32), axis=0, keepdims=True)
+    route_ref[0:1] = source_ref[...] * 8
+    route_ref[1:2] = target * ROWS_PER_PEER + rank * NF
+    peers = label_ref.shape[0]
+    to_peer = lax.broadcasted_iota(jnp.int32, (peers, EPD), 0) == target
+    lane = lax.broadcasted_iota(jnp.int32, (peers, BLK), 1)
+    label = jnp.full((peers, BLK), -1.0, jnp.float32)
+    value = block_ref[...].astype(jnp.float32) + 1.0
+    for k in range(CAP):
+        named = jnp.where(to_peer & (rank == k), value, 0.0)
+        label = jnp.where(lane == k, jnp.sum(named, axis=1, keepdims=True) - 1.0, label)
+    label_ref[...] = label
+
+    tile.wait()
+    lane = lax.broadcasted_iota(jnp.int32, (CX, BLK), 1) // HALO
+    left = jnp.zeros((CX, BLK), jnp.float32)
+    right = jnp.zeros((CX, BLK), jnp.float32)
     for level in range(LEV):
-        own = jnp.concatenate([x_ref[level], bottom_ref[level], top_ref[level]], axis=0)
-        left = jnp.where(lane == level, pltpu.roll(own[:, :BLK], HALO * level, 1), left)
-        right = jnp.where(
-            lane == level, pltpu.roll(own[:, CY - BLK :], (HALO * level + HALO) % BLK, 1), right
-        )
+        left, right = packed(x_buf[level], left, right, lane, level)
     left_ref[...] = left
     right_ref[...] = right
 
-
-def split_kernel(w_ref, *refs):
-    high_ref, low_ref = refs[-2:]
-    rows = pl.ds(pl.program_id(0) * CHUNK, CHUNK)
-    weight = w_ref[...]
-    high = weight.astype(jnp.bfloat16)
-    high_ref[rows] = high
-    low_ref[rows] = (weight - high.astype(jnp.float32)).astype(jnp.bfloat16)
+    @pl.loop(0, N_CHUNKS)
+    def _(part):
+        fetch(part).wait()
+        for k in range(CHUNK):
+            weight = w_buf[part * CHUNK + k]
+            high = weight.astype(jnp.bfloat16)
+            low = (weight - high.astype(jnp.float32)).astype(jnp.bfloat16)
+            pair = part * (CHUNK // 2) + k // 2
+            rows = slice(k % 2 * BLK, (k % 2 + 1) * BLK)
+            halves_ref[pair, rows, :BLK] = high
+            halves_ref[pair, rows, BLK:] = low
+
+
+def packed(rows, left, right, lane, level):
+    left = jnp.where(lane == level, pltpu.roll(rows[:, :BLK], HALO * level, 1), left)
+    shift = (HALO * level + HALO) % BLK
+    right = jnp.where(lane == level, pltpu.roll(rows[:, CY - BLK :], shift, 1), right)
+    return left, right
+
+
+def pack_kernel(top_ref, bottom_ref, left_in, right_in, left_ref, right_ref):
+    lane = lax.broadcasted_iota(jnp.int32, (2 * HALO, BLK), 1) // HALO
+    left = jnp.zeros((2 * HALO, BLK), jnp.float32)
+    right = jnp.zeros((2 * HALO, BLK), jnp.float32)
+    for level in range(LEV):
+        rows = jnp.concatenate([bottom_ref[level], top_ref[level]], axis=0)
+        left, right = packed(rows, left, right, lane, level)
+    left_ref[:CX] = left_in[...]
+    left_ref[CX:] = left
+    right_ref[:CX] = right_in[...]
+    right_ref[CX:] = right
 
 
 def surface_kernel(
-    meta_ref, rates_ref, route_ref, x_ref, top_ref, bottom_ref, left_ref, right_ref, label_ref,
-    high_ref, low_ref, slots_ref, surface_ref, blocks, keep_ref,
+    meta_ref, diffusion_ref, courant_ref, route_ref, x_ref, top_ref, bottom_ref, left_ref, right_ref, label_ref,
+    halves_ref, slots_ref, surface_ref, blocks, keep_ref,
 ):
     slots_ref[...] = jnp.zeros(slots_ref.shape, jnp.float32)
     slots_ref[pl.ds(ROWS_PER_PEER - 1, label_ref.shape[0], stride=ROWS_PER_PEER), :] = label_ref[...]
@@ -91,7 +144,7 @@
         field = extended(
             x_ref[level], top_ref[level], bottom_ref[level], left_ref[...], right_ref[...], level
         )
-        field = evolve(field, keep_ref[...], rates_ref[0, level], rates_ref[1, level], meta_ref[4])
+        field = evolve(field, keep_ref[...], diffusion_ref[0, level], courant_ref[0, level], meta_ref[4])
         field = field[:CX, :CY]
         surface_ref[level] = field
         high = field.astype(jnp.bfloat16).astype(jnp.float32)
@@ -101,21 +154,30 @@
             blocks[pl.ds(half * 8 + level, CX, stride=16), :] = high[:, cols]
             blocks[pl.ds(half * 8 + NF + level, CX, stride=16), :] = low[:, cols]
 
-    def entry(e):
-        picked = blocks[pl.ds(pl.multiple_of(route_ref[0, e] * 8, 8), 8), :].astype(jnp.bfloat16)
-        dims = (((1,), (1,)), ((), ()))
-        both = lax.dot_general(picked, high_ref[e], dims, preferred_element_type=jnp.float32)
-        both += lax.dot_general(picked, low_ref[e], dims, preferred_element_type=jnp.float32)
-        slots_ref[pl.ds(route_ref[1, e], NF), :] = both[:NF] + both[NF:]
-
-    @pl.loop(0, N_CHUNKS)
-    def _(part):
-        for k in range(CHUNK):
-            entry(part * CHUNK + k)
+    def pair(p):
+        def picked(e):
+            return blocks[pl.ds(pl.multiple_of(route_ref[0, e], 8), 8), :]
+
+        rows = jnp.concatenate([picked(2 * p), picked(2 * p + 1)], axis=0).astype(jnp.bfloat16)
+        both = lax.dot_general(
+            jnp.concatenate([rows, rows], axis=1),
+            halves_ref[p],
+            (((1,), (1,)), ((), ())),
+            preferred_element_type=jnp.float32,
+        )
+        one = both[0:8, :BLK]
+        two = both[8:16, BLK:]
+        slots_ref[pl.ds(route_ref[1, 2 * p], NF), :] = one[:NF] + one[NF:]
+        slots_ref[pl.ds(route_ref[1, 2 * p + 1], NF), :] = two[:NF] + two[NF:]
+
+    @pl.loop(0, EPD // 2, step=UNROLL)
+    def _(start):
+        for k in range(UNROLL):
+            pair(start + k)
 
 
 def aloft_kernel(
-    meta_ref, rates_ref, x_ref, top_ref, bottom_ref, left_ref, right_ref, out_ref, keep_ref
+    meta_ref, diffusion_ref, courant_ref, x_ref, top_ref, bottom_ref, left_ref, right_ref, out_ref, keep_ref
 ):
     group = pl.program_id(0) + 1
 
@@ -128,7 +190,7 @@
         field = extended(
             x_ref[k], top_ref[k], bottom_ref[k], left_ref[...], right_ref[...], level
         )
-        field = evolve(field, keep_ref[...], rates_ref[0, level], rates_ref[1, level], meta_ref[4])
+        field = evolve(field, keep_ref[...], diffusion_ref[0, level], courant_ref[0, level], meta_ref[4])
         out_ref[k] = field[:CX, :CY]
 
 
@@ -163,6 +225,7 @@
     x = air_sea_state[0]
     smem = pl.BlockSpec(memory_space=pltpu.SMEM)
     vmem = pl.BlockSpec(memory_space=pltpu.VMEM)
+    anywhere = pl.BlockSpec(memory_space=pl.ANY)
 
     def limit(mib):
         return pltpu.CompilerParams(vmem_limit_bytes=mib << 20)
@@ -176,44 +239,45 @@
             jnp.where(lax.axis_index("sec") == 0, STEPS_A, STEPS_O),
         ]
     ).astype(jnp.int32)
-    rates = jnp.concatenate([diffusion, courant], axis=0)
-
-    with jax.named_scope("routes"):
-        target = dest_peer[0][:, 0]
-        entry = jnp.arange(EPD, dtype=jnp.int32)
-        earlier = (target[:, None] == target[None, :]) & (entry[None, :] < entry[:, None])
-        rank = jnp.sum(earlier.astype(jnp.int32), axis=1)
-        route = jnp.stack([src_block[0], target * ROWS_PER_PEER + rank * NF])
-        to_peer = target[None, :] == jnp.arange(peers, dtype=jnp.int32)[:, None]
-        label = [
-            jnp.sum(jnp.where(to_peer & (rank == k)[None, :], dest_block[0][None, :] + 1, 0), axis=1)
-            for k in range(CAP)
-        ]
-        label = jnp.stack(label, axis=1).astype(jnp.float32) - 1.0
-        label = jnp.pad(label, ((0, 0), (0, BLK - CAP)), constant_values=-1.0)
-
-    with jax.named_scope("split"):
-        part = pl.BlockSpec((CHUNK, BLK, BLK), lambda i: (i, 0, 0))
-        half = pltpu.VMEM((EPD, BLK, BLK), jnp.bfloat16)
-        high, low = pl.pallas_call(
-            split_kernel,
-            grid=(N_CHUNKS,),
-            in_specs=[part] + [pl.BlockSpec(memory_space=pl.ANY)] * 4,
-            out_specs=[vmem, vmem],
-            out_shape=(half, half),
-            compiler_params=limit(6),
-            name="split",
-        )(
-            pltpu.with_memory_space_constraint(remap_weight[0], pltpu.HBM), meta, rates, route, label
-        )
-
     with jax.named_scope("halo"):
         top = lax.ppermute(x[:, CX - HALO :], "gx", ring("gx", 1))
         bottom = lax.ppermute(x[:, :HALO], "gx", ring("gx", -1))
+
+    with jax.named_scope("prepare"):
+        centre = jax.ShapeDtypeStruct((CX, BLK), jnp.float32)
+        halves, route, label, left, right = pl.pallas_call(
+            prepare_kernel,
+            in_specs=[anywhere, anywhere, vmem, vmem, vmem, anywhere],
+            out_specs=[vmem] * 5,
+            out_shape=(
+                pltpu.VMEM((EPD // 2, 2 * BLK, 2 * BLK), jnp.bfloat16),
+                jax.ShapeDtypeStruct((2, EPD), jnp.int32),
+                jax.ShapeDtypeStruct((peers, BLK), jnp.float32),
+                centre,
+                centre,
+            ),
+            scratch_shapes=[
+                pltpu.VMEM((EPD, BLK, BLK), jnp.float32),
+                pltpu.VMEM((LEV, CX, CY), jnp.float32),
+                pltpu.SemaphoreType.DMA((N_CHUNKS,)),
+                pltpu.SemaphoreType.DMA,
+            ],
+            compiler_params=limit(18),
+            name="prepare",
+        )(
+            pltpu.with_memory_space_constraint(remap_weight[0], pltpu.HBM),
+            pltpu.with_memory_space_constraint(x, pltpu.HBM),
+            src_block,
+            dest_peer.reshape(1, EPD),
+            dest_block,
+            meta,
+        )
+
+    with jax.named_scope("halo"):
         side = jax.ShapeDtypeStruct((ROWS, BLK), jnp.float32)
         left, right = pl.pallas_call(
-            pack_kernel, out_shape=(side, side), compiler_params=limit(3), name="pack"
-        )(x, top, bottom)
+            pack_kernel, out_shape=(side, side), compiler_params=limit(2), name="pack"
+        )(top, bottom, left, right)
         from_right = lax.ppermute(left, "gy", ring("gy", -1))
         from_left = lax.ppermute(right, "gy", ring("gy", 1))
 
@@ -224,8 +288,8 @@
         surface_kernel,
         grid=(1,),
         in_specs=[
-            smem, smem, smem, tile, edge, edge, whole, whole,
-            pl.BlockSpec((peers, BLK), lambda i: (0, 0)), vmem, vmem,
+            smem, smem, smem, smem, tile, edge, edge, whole, whole,
+            pl.BlockSpec((peers, BLK), lambda i: (0, 0)), vmem,
         ],
         out_specs=[pl.BlockSpec((rows_out, BLK), lambda i: (0, 0)), tile],
         out_shape=(
@@ -238,25 +302,28 @@
         ],
         compiler_params=limit(6),
         name="surface",
-    )(meta, rates, route, x, top, bottom, from_left, from_right, label, high, low)
+    )(
+        meta, diffusion, courant, route, x, top, bottom, from_left, from_right, label, halves
+    )
 
     tile_up = pl.BlockSpec((NF, CX, CY), lambda i: (i + 1, 0, 0))
     edge_up = pl.BlockSpec((NF, HALO, CY), lambda i: (i + 1, 0, 0))
     aloft = pl.pallas_call(
         aloft_kernel,
         grid=(LEV // NF - 1,),
-        in_specs=[smem, smem, tile_up, edge_up, edge_up, whole, whole],
+        in_specs=[smem, smem, smem, tile_up, edge_up, edge_up, whole, whole],
         out_specs=tile_up,
         out_shape=jax.ShapeDtypeStruct((LEV, CX, CY), jnp.float32),
         scratch_shapes=[pltpu.VMEM((ROWS, COLS), jnp.float32)],
         compiler_params=limit(4),
         name="aloft",
-    )(meta, rates, x, top, bottom, from_left, from_right)
-
+    )(meta, diffusion, courant, x, top, bottom, from_left, from_right)
+
+    outgoing = lax.ppermute(outgoing, "sec", ring("sec", 1))
     incoming = lax.all_to_all(
         outgoing.reshape(peers, ROWS_PER_PEER, 1, BLK), ("gx", "gy"), split_axis=0, concat_axis=0, tiled=True
     )
-    incoming = lax.ppermute(incoming.reshape(rows_out, BLK), "sec", ring("sec", 1))
+    incoming = incoming.reshape(rows_out, BLK)
 
     new_state, remapped = pl.pallas_call(
         finish_kernel,

time: 87.2 us -> 75.5 us (0.87)
  the two profiles are of different devices: /device:TPU:8 before, /device:TPU:1 now
where the time goes in v3:
time: 75.5 us; the launch traced here: 74.6 us
  starting transfers between devices  26.5 us (35%)
  Pallas kernels  22.7 us (30%)
  waiting for transfers between devices  21.4 us (28%)
  local copies, waits for them, and re-layouts  3.2 us (4%)
    all_to_all x1, waiting for transfers between devices, body(): lax.all_to_all(outgoing.reshape(peers, ROWS_PER_PEER, 1, BLK), ('gx', 'gy...  18.1 us
    all_to_all x1, starting transfers between devices, body(): lax.all_to_all(outgoing.reshape(peers, ROWS_PER_PEER, 1, BLK), ('gx', 'gy...  11.4 us
    pallas_call x1, Pallas kernels, body(): pl.pallas_call(surface_kernel, grid=(1,), in_specs=[smem, smem, smem, sme...  7.23 us
    pallas_call x1, Pallas kernels, body(): pl.pallas_call(aloft_kernel, grid=(LEV // NF - 1,), in_specs=[smem, smem,...  7.15 us
    pallas_call x1, Pallas kernels, body(): pl.pallas_call(prepare_kernel, in_specs=[anywhere, anywhere, vmem, vmem,...  7.08 us
    ppermute x1, starting transfers between devices, body(): bottom = lax.ppermute(x[:, :HALO], 'gx', ring('gx', -1))  6.48 us
    ppermute x1, starting transfers between devices, body(): from_right = lax.ppermute(left, 'gy', ring('gy', -1))  3.81 us
    ppermute x1, starting transfers between devices, body(): outgoing = lax.ppermute(outgoing, 'sec', ring('sec', 1))  3.57 us
  transfers between devices with their start and end apart: 6, of which 3 were waited for; matrix products, arithmetic and copies ran while one was open for 0% of the time, Pallas kernels for 19%

profile of v3, /device:TPU:1, one launch (start us, length us, event | category | flops | bytes accessed | tf_op | source)
XLA Modules:
  0.0 74.6 jit_solution(11107792894173177844)
XLA Ops:
  0.6 0.0 copy-start
  0.6 0.0 copy-start.3
  0.7 0.0 copy-start.2
  0.7 1.1 %fusion = (f32[16,8,256]{2,1,0:T(8,128)S(1)}, f32[16,8,256]{2,1,0:T(8,128)S(1)}) fusion(f32[16,48,256]{2,1,0:T(8,128)} %bitcast.11), kind=kLoop, calls=%fused_computation | loop fusion | bytes 524288 | tf_op jit(solution)/shard_map/halo/slice | solution.py:244
  1.7 6.5 %collective-permute-start.1 = (f32[16,8,256]{2,1,0:T(8,128)S(1)}, f32[16,8,256]{2,1,0:T(8,128)S(1)}, u32[]{:S(2)}, u32[]{:S(2)}) collective-permute-start(f32[16,8,256]{2,1,0:T(8,128)S(1)} %get-tuple-element.24), channel_id=1, source_target_pairs={{0,112},{16,0},{32,16},{48,32},{64,48},{80,64},{96,80},{112,96},{1... | collective-permute-start | bytes 393224 | tf_op jit(solution)/shard_map/halo/ppermute | solution.py:244
  8.2 0.0 collective-permute-start
  8.2 0.1 stack.15.meta_ref
  8.3 0.0 copy-start.4
  8.3 0.7 copy-done.4
  9.0 0.0 copy-start.5
  9.0 0.7 copy-done.5
  9.7 0.0 copy-start.6
  9.7 0.7 copy-done.6
  10.3 7.1 %prepare.1 = (bf16[96,256,256]{2,1,0:T(8,128)(2,1)S(1)}, s32[2,192]{1,0:T(2,128)S(1)}, f32[128,128]{1,0:T(8,128)S(1)}, f32[48,128]{1,0:T(8,128)S(1)}, f32[48,128]{1,0:T(8,128)S(1)}) custom-call(f32[192,128,128]{2,1,0:T(8,128)} %bitcast.18, f32[16,48,256]{2,1,0:T(8,128)} %bitcast.12, s32[1,192]{1,0:T(1,128)S(1)} %copy-done.4, s32[1,192]{1,0:T(1,128)S(1)} %bitcast.17, ...), custom_call_target="tpu_custom_call" | custom-call | tf_op jit(solution)/shard_map/prepare/prepare/pallas_call | solution.py:248
  17.4 0.0 collective-permute-done.1.bottom_ref
  17.4 0.0 collective-permute-done.top_ref
  17.4 0.1 pack.1
  17.6 1.3 %collective-permute-start.2 = (f32[64,128]{1,0:T(8,128)S(1)}, f32[64,128]{1,0:T(8,128)S(1)}, u32[]{:S(2)}, u32[]{:S(2)}) collective-permute-start(f32[64,128]{1,0:T(8,128)S(1)} %get-tuple-element.16), channel_id=1, source_target_pairs={{0,1},{1,2},{2,3},{3,4},{4,5},{5,6},{6,7},{7,8},{8,9},{9,10},{10,1... | collective-permute-start | bytes 98312 | tf_op jit(solution)/shard_map/halo/ppermute | solution.py:282
  18.9 3.8 %collective-permute-start.3 = (f32[64,128]{1,0:T(8,128)S(1)}, f32[64,128]{1,0:T(8,128)S(1)}, u32[]{:S(2)}, u32[]{:S(2)}) collective-permute-start(f32[64,128]{1,0:T(8,128)S(1)} %get-tuple-element.17), channel_id=1, source_target_pairs={{0,15},{1,0},{2,1},{3,2},{4,3},{5,4},{6,5},{7,6},{8,7},{9,8},{10,9... | collective-permute-start | bytes 98312 | tf_op jit(solution)/shard_map/halo/ppermute | solution.py:281
  22.7 1.2 %collective-permute-done.2.left_ref = f32[64,128]{1,0:T(8,128)S(1)} collective-permute-done((f32[64,128]{1,0:T(8,128)S(1)}, f32[64,128]{1,0:T(8,128)S(1)}, u32[]{:S(2)}, u32[]{:S(2)}) %collective-permute-start.2) | collective-permute-done | bytes 32800 | tf_op jit(solution)/shard_map/halo/ppermute | solution.py:282
  23.9 0.0 collective-permute-done.3.right_ref
  23.9 0.0 copy-done
  23.9 0.0 copy-done.3
  23.9 0.0 copy-done.2
  23.9 7.2 %surface.1 = (f32[1664,128]{1,0:T(8,128)S(1)}, f32[4,48,256]{2,1,0:T(8,128)S(1)}) custom-call(s32[5]{0:T(128)S(1)} %stack.15.meta_ref, f32[1,16]{1,0:T(1,128)S(1)} %copy-done.2, f32[1,16]{1,0:T(1,128)S(1)} %copy-done.3, s32[2,192]{1,0:T(2,128)S(1)} %get-tuple-element.13.route_ref, f32[16,48,256]{2,1,0:T(8,128)S(1)} %bitcast.13, ...), custom_call_target="tpu_custom_call" | custom-call | tf_op jit(solution)/shard_map/surface/pallas_call | solution.py:287
  31.1 3.6 %collective-permute-start.4 = (f32[1664,128]{1,0:T(8,128)S(1)}, f32[1664,128]{1,0:T(8,128)}, u32[]{:S(2)}, u32[]{:S(2)}) collective-permute-start(f32[1664,128]{1,0:T(8,128)S(1)} %get-tuple-element.20), channel_id=1, source_target_pairs={{0,128},{128,0},{1,129},{129,1},{2,130},{130,2},{3,131},{131,3},{4... | collective-permute-start | bytes 2555912 | tf_op jit(solution)/shard_map/ppermute | solution.py:322
  34.7 2.1 %collective-permute-done.4 = f32[1664,128]{1,0:T(8,128)} collective-permute-done((f32[1664,128]{1,0:T(8,128)S(1)}, f32[1664,128]{1,0:T(8,128)}, u32[]{:S(2)}, u32[]{:S(2)}) %collective-permute-start.4) | collective-permute-done | bytes 852000 | tf_op jit(solution)/shard_map/ppermute | solution.py:322
  36.8 11.4 %all-to-all-start = ((f32[128,13,1,128]{3,2,1,0:T(1,128)}), f32[128,13,1,128]{3,2,1,0:T(1,128)S(1)}, u32[]{:S(2)}, u32[]{:S(2)}) async-start(f32[128,13,1,128]{3,2,1,0:T(1,128)} %bitcast.6), calls=%async_computation | async-start | bytes 1703936 | tf_op jit(solution)/shard_map/all_to_all | solution.py:323
  48.2 7.1 %aloft.1.aloft_ref = f32[16,48,256]{2,1,0:T(8,128)} custom-call(s32[5]{0:T(128)S(1)} %stack.15.meta_ref, f32[1,16]{1,0:T(1,128)S(1)} %copy-done.2, f32[1,16]{1,0:T(1,128)S(1)} %copy-done.3, f32[16,48,256]{2,1,0:T(8,128)S(1)} %bitcast.14, f32[16,8,256]{2,1,0:T(8,128)S(1)} %collective-permute-done.top_ref, ...), custom_call_target="tpu_custom_call" | custom-call | tf_op jit(solution)/shard_map/aloft/pallas_call | solution.py:311
  55.4 18.1 %all-to-all-done = f32[128,13,1,128]{3,2,1,0:T(1,128)S(1)} async-done(((f32[128,13,1,128]{3,2,1,0:T(1,128)}), f32[128,13,1,128]{3,2,1,0:T(1,128)S(1)}, u32[]{:S(2)}, u32[]{:S(2)}) %all-to-all-start) | async-done | bytes 852000 | tf_op jit(solution)/shard_map/all_to_all | solution.py:323
  73.5 0.0 copy-done.1
  73.5 1.2 %finish.1 = (f32[16,48,256]{2,1,0:T(8,128)}, f32[4,48,256]{2,1,0:T(8,128)}) custom-call(f32[1664,128]{1,0:T(8,128)S(1)} %bitcast.15, f32[4,48,256]{2,1,0:T(8,128)S(1)} %get-tuple-element.21.surface_ref, f32[48,256]{1,0:T(8,128)S(1)} %bitcast.16, f32[16,48,256]{2,1,0:T(8,128)} %aloft.1.aloft_ref), custom_call_target="tpu_custom_call", output_to_operand_aliasing={{0}: (3, {})} | custom-call | tf_op jit(solution)/shard_map/finish/pallas_call | solution.py:328
  (1 shorter events, 0.0 us)
Async XLA Ops:
  0.6 23.3 %copy-start = (f32[1,16,48,256]{3,2,1,0:T(8,128)S(1)}, f32[1,16,48,256]{3,2,1,0:T(8,128)}, u32[]{:S(2)}) copy-start(f32[1,16,48,256]{3,2,1,0:T(8,128)} %param.8) | copy-start | bytes 2359300
  0.6 23.3 %copy-start.3 = (f32[1,16]{1,0:T(1,128)S(1)}, f32[1,16]{1,0:T(1,128)}, u32[]{:S(2)}) copy-start(f32[1,16]{1,0:T(1,128)} %courant_ref.3) | copy-start | bytes 196
  0.7 23.2 %copy-start.2 = (f32[1,16]{1,0:T(1,128)S(1)}, f32[1,16]{1,0:T(1,128)}, u32[]{:S(2)}) copy-start(f32[1,16]{1,0:T(1,128)} %diffusion_ref.3) | copy-start | bytes 196
  1.7 15.7 %collective-permute-start.1 = (f32[16,8,256]{2,1,0:T(8,128)S(1)}, f32[16,8,256]{2,1,0:T(8,128)S(1)}, u32[]{:S(2)}, u32[]{:S(2)}) collective-permute-start(f32[16,8,256]{2,1,0:T(8,128)S(1)} %get-tuple-element.24), channel_id=1, source_target_pairs={{0,112},{16,0},{32,16},{48,32},{64,48},{80,64},{96,80},{112,96},{1... | collective-permute-start | bytes 393224 | tf_op jit(solution)/shard_map/halo/ppermute | solution.py:244
  8.2 9.2 %collective-permute-start = (f32[16,8,256]{2,1,0:T(8,128)S(1)}, f32[16,8,256]{2,1,0:T(8,128)S(1)}, u32[]{:S(2)}, u32[]{:S(2)}) collective-permute-start(f32[16,8,256]{2,1,0:T(8,128)S(1)} %get-tuple-element.25), channel_id=1, source_target_pairs={{0,16},{16,32},{32,48},{48,64},{64,80},{80,96},{96,112},{112,0},{1... | collective-permute-start | bytes 393224 | tf_op jit(solution)/shard_map/halo/ppermute | solution.py:243
  8.3 0.7 copy-start.4
  9.0 0.7 copy-start.5
  9.7 0.7 copy-start.6
  10.3 63.1 %copy-start.1 = (f32[1,48,256]{2,1,0:T(8,128)S(1)}, f32[1,48,256]{2,1,0:T(8,128)}, u32[]{:S(2)}) copy-start(f32[1,48,256]{2,1,0:T(8,128)} %param.11) | copy-start | bytes 147460
  17.6 6.3 %collective-permute-start.2 = (f32[64,128]{1,0:T(8,128)S(1)}, f32[64,128]{1,0:T(8,128)S(1)}, u32[]{:S(2)}, u32[]{:S(2)}) collective-permute-start(f32[64,128]{1,0:T(8,128)S(1)} %get-tuple-element.16), channel_id=1, source_target_pairs={{0,1},{1,2},{2,3},{3,4},{4,5},{5,6},{6,7},{7,8},{8,9},{9,10},{10,1... | collective-permute-start | bytes 98312 | tf_op jit(solution)/shard_map/halo/ppermute | solution.py:282
  18.9 5.0 %collective-permute-start.3 = (f32[64,128]{1,0:T(8,128)S(1)}, f32[64,128]{1,0:T(8,128)S(1)}, u32[]{:S(2)}, u32[]{:S(2)}) collective-permute-start(f32[64,128]{1,0:T(8,128)S(1)} %get-tuple-element.17), channel_id=1, source_target_pairs={{0,15},{1,0},{2,1},{3,2},{4,3},{5,4},{6,5},{7,6},{8,7},{9,8},{10,9... | collective-permute-start | bytes 98312 | tf_op jit(solution)/shard_map/halo/ppermute | solution.py:281
  31.1 5.7 %collective-permute-start.4 = (f32[1664,128]{1,0:T(8,128)S(1)}, f32[1664,128]{1,0:T(8,128)}, u32[]{:S(2)}, u32[]{:S(2)}) collective-permute-start(f32[1664,128]{1,0:T(8,128)S(1)} %get-tuple-element.20), channel_id=1, source_target_pairs={{0,128},{128,0},{1,129},{129,1},{2,130},{130,2},{3,131},{131,3},{4... | collective-permute-start | bytes 2555912 | tf_op jit(solution)/shard_map/ppermute | solution.py:322
  36.8 36.6 %all-to-all-start = ((f32[128,13,1,128]{3,2,1,0:T(1,128)}), f32[128,13,1,128]{3,2,1,0:T(1,128)S(1)}, u32[]{:S(2)}, u32[]{:S(2)}) async-start(f32[128,13,1,128]{3,2,1,0:T(1,128)} %bitcast.6), calls=%async_computation | async-start | bytes 1703936 | tf_op jit(solution)/shard_map/all_to_all | solution.py:323

commit v4 on v3

--- a/solution.py
+++ b/solution.py
@@ -21,7 +21,9 @@
 CHUNK = 16
 N_CHUNKS = EPD // CHUNK
 ROWS_PER_PEER = CAP * NF + 1
-UNROLL = 8
+UNROLL = 36
+LATER = 3
+DEPTH = 4
 
 
 def ring(axis, shift):
@@ -46,51 +48,72 @@
     return jnp.concatenate([own, beyond], axis=1)
 
 
-def evolve(field, keep, diffuse, carry_rate, steps):
-    field = field * keep
-    centre = 1.0 - 4.0 * diffuse - carry_rate
-    upwind = diffuse + carry_rate
-
-    def step(_, u):
+def evolve(fields, keep_ref, rates, steps):
+    def step(u, diffuse, carry_rate):
         beside = pltpu.roll(u, ROWS - 1, 0) + pltpu.roll(u, 1, 1) + pltpu.roll(u, COLS - 1, 1)
-        return (centre * u + upwind * pltpu.roll(u, 1, 0) + diffuse * beside) * keep
-
-    return lax.fori_loop(0, steps, step, field)
-
-
-def prepare_kernel(
-    w_ref, x_ref, source_ref, peer_ref, block_ref, meta_ref,
-    halves_ref, route_ref, label_ref, left_ref, right_ref, w_buf, x_buf, w_sems, x_sem,
-):
+        upwind = (diffuse + carry_rate) * pltpu.roll(u, 1, 0)
+        centre = (1.0 - 4.0 * diffuse - carry_rate) * u
+        return (centre + upwind + diffuse * beside) * keep_ref[...]
+
+    def advance(_, now):
+        for _ in range(STEPS_O):
+            now = tuple(step(u, *rate) for u, rate in zip(now, rates))
+        return now
+
+    fields = tuple(u * keep_ref[...] for u in fields)
+    return lax.fori_loop(0, steps // STEPS_O, advance, fields)
+
+
+def extended_group(meta_ref, rate_refs, x_ref, top_ref, bottom_ref, left_ref, right_ref, keep_ref, first):
+    fields, rates = [], []
+    for k in range(NF):
+        fields.append(
+            extended(x_ref[k], top_ref[k], bottom_ref[k], left_ref[...], right_ref[...], first + k)
+        )
+        rates.append(tuple(ref[0, first + k] for ref in rate_refs))
+    fields = evolve(fields, keep_ref, rates, meta_ref[4])
+    return [u[:CX, :CY] for u in fields]
+
+
+def split_parts(w_ref, w_buf, sems, halves_ref, first):
     def fetch(part):
         rows = pl.ds(part * CHUNK, CHUNK)
-        return pltpu.make_async_copy(w_ref.at[rows], w_buf.at[rows], w_sems.at[part])
-
+        whence = w_ref.at[pl.ds((first + part) * CHUNK, CHUNK)]
+        return pltpu.make_async_copy(whence, w_buf.at[rows], sems.at[part])
+
+    def begin():
+        for part in range(min(DEPTH, sems.shape[0])):
+            fetch(part).start()
+
+    def finish():
+        @pl.loop(0, sems.shape[0])
+        def _(part):
+            fetch(part).wait()
+
+            @pl.when(part + DEPTH < sems.shape[0])
+            def _():
+                fetch(part + DEPTH).start()
+
+            for k in range(CHUNK):
+                weight = w_buf[part * CHUNK + k].T
+                high = weight.astype(jnp.bfloat16)
+                low = (weight - high.astype(jnp.float32)).astype(jnp.bfloat16)
+                pair = part * (CHUNK // 2) + k // 2
+                cols = slice(k % 2 * BLK, (k % 2 + 1) * BLK)
+                halves_ref[pair, :BLK, cols] = high
+                halves_ref[pair, BLK:, cols] = low
+
+    return begin, finish
+
+
+def prepare_kernel(
+    w_ref, x_ref, meta_ref, halves_ref, left_ref, right_ref, w_buf, x_buf, w_sems, x_sem
+):
+    del meta_ref
     tile = pltpu.make_async_copy(x_ref, x_buf, x_sem)
-    for part in range(2):
-        fetch(part).start()
     tile.start()
-    for part in range(2, N_CHUNKS):
-        fetch(part).start()
-
-    target = peer_ref[...]
-    same = jnp.broadcast_to(target.astype(jnp.float32), (EPD, EPD))
-    same = same == same.T
-    first = lax.broadcasted_iota(jnp.int32, (EPD, EPD), 0)
-    second = lax.broadcasted_iota(jnp.int32, (EPD, EPD), 1)
-    rank = jnp.sum((same & (first < second)).astype(jnp.int32), axis=0, keepdims=True)
-    route_ref[0:1] = source_ref[...] * 8
-    route_ref[1:2] = target * ROWS_PER_PEER + rank * NF
-    peers = label_ref.shape[0]
-    to_peer = lax.broadcasted_iota(jnp.int32, (peers, EPD), 0) == target
-    lane = lax.broadcasted_iota(jnp.int32, (peers, BLK), 1)
-    label = jnp.full((peers, BLK), -1.0, jnp.float32)
-    value = block_ref[...].astype(jnp.float32) + 1.0
-    for k in range(CAP):
-        named = jnp.where(to_peer & (rank == k), value, 0.0)
-        label = jnp.where(lane == k, jnp.sum(named, axis=1, keepdims=True) - 1.0, label)
-    label_ref[...] = label
-
+    begin, finish = split_parts(w_ref, w_buf, w_sems, halves_ref, 0)
+    begin()
     tile.wait()
     lane = lax.broadcasted_iota(jnp.int32, (CX, BLK), 1) // HALO
     left = jnp.zeros((CX, BLK), jnp.float32)
@@ -99,18 +122,34 @@
         left, right = packed(x_buf[level], left, right, lane, level)
     left_ref[...] = left
     right_ref[...] = right
-
-    @pl.loop(0, N_CHUNKS)
-    def _(part):
-        fetch(part).wait()
-        for k in range(CHUNK):
-            weight = w_buf[part * CHUNK + k]
-            high = weight.astype(jnp.bfloat16)
-            low = (weight - high.astype(jnp.float32)).astype(jnp.bfloat16)
-            pair = part * (CHUNK // 2) + k // 2
-            rows = slice(k % 2 * BLK, (k % 2 + 1) * BLK)
-            halves_ref[pair, rows, :BLK] = high
-            halves_ref[pair, rows, BLK:] = low
+    finish()
+
+
+def route_kernel(
+    w_ref, source_ref, peer_ref, block_ref, after_ref, halves_ref, route_ref, label_ref, w_buf, sems
+):
+    del after_ref
+    begin, finish = split_parts(w_ref, w_buf, sems, halves_ref, N_CHUNKS - sems.shape[0])
+    begin()
+    target = peer_ref[...]
+    column = jnp.broadcast_to(target.astype(jnp.float32), (8, EPD)).T[:, :1].astype(jnp.int32)
+    first = lax.broadcasted_iota(jnp.int32, (EPD, EPD), 0)
+    second = lax.broadcasted_iota(jnp.int32, (EPD, EPD), 1)
+    earlier = (column == target) & (first < second)
+    rank = jnp.sum(earlier.astype(jnp.int32), axis=0, keepdims=True)
+    route_ref[0:1] = source_ref[...] * 8
+    route_ref[1:2] = target * ROWS_PER_PEER + rank * NF
+    peers = label_ref.shape[0]
+    to_peer = lax.broadcasted_iota(jnp.int32, (peers, EPD), 0) == target
+    slot = lax.broadcasted_iota(jnp.int32, (BLK, EPD), 0) == rank
+    value = jnp.where(slot, block_ref[...].astype(jnp.float32) + 1.0, 0.0)
+    label_ref[...] = lax.dot_general(
+        to_peer.astype(jnp.bfloat16),
+        value.astype(jnp.bfloat16),
+        (((1,), (1,)), ((), ())),
+        preferred_element_type=jnp.float32,
+    ) - 1.0
+    finish()
 
 
 def packed(rows, left, right, lane, level):
@@ -135,17 +174,16 @@
 
 def surface_kernel(
     meta_ref, diffusion_ref, courant_ref, route_ref, x_ref, top_ref, bottom_ref, left_ref, right_ref, label_ref,
-    halves_ref, slots_ref, surface_ref, blocks, keep_ref,
+    halves_ref, later_ref, slots_ref, surface_ref, blocks, keep_ref,
 ):
     slots_ref[...] = jnp.zeros(slots_ref.shape, jnp.float32)
     slots_ref[pl.ds(ROWS_PER_PEER - 1, label_ref.shape[0], stride=ROWS_PER_PEER), :] = label_ref[...]
     keep_ref[...] = inside(meta_ref).astype(jnp.float32)
-    for level in range(NF):
-        field = extended(
-            x_ref[level], top_ref[level], bottom_ref[level], left_ref[...], right_ref[...], level
-        )
-        field = evolve(field, keep_ref[...], diffusion_ref[0, level], courant_ref[0, level], meta_ref[4])
-        field = field[:CX, :CY]
+    fields = extended_group(
+        meta_ref, (diffusion_ref, courant_ref), x_ref, top_ref, bottom_ref, left_ref, right_ref,
+        keep_ref, 0,
+    )
+    for level, field in enumerate(fields):
         surface_ref[level] = field
         high = field.astype(jnp.bfloat16).astype(jnp.float32)
         low = field - high
@@ -154,26 +192,28 @@
             blocks[pl.ds(half * 8 + level, CX, stride=16), :] = high[:, cols]
             blocks[pl.ds(half * 8 + NF + level, CX, stride=16), :] = low[:, cols]
 
-    def pair(p):
+    def pair(ref, p, first):
         def picked(e):
             return blocks[pl.ds(pl.multiple_of(route_ref[0, e], 8), 8), :]
 
-        rows = jnp.concatenate([picked(2 * p), picked(2 * p + 1)], axis=0).astype(jnp.bfloat16)
-        both = lax.dot_general(
-            jnp.concatenate([rows, rows], axis=1),
-            halves_ref[p],
-            (((1,), (1,)), ((), ())),
-            preferred_element_type=jnp.float32,
+        e = 2 * (p + first)
+        rows = jnp.concatenate([picked(e), picked(e + 1)], axis=0).astype(jnp.bfloat16)
+        both = jnp.dot(
+            jnp.concatenate([rows, rows], axis=1), ref[p], preferred_element_type=jnp.float32
         )
         one = both[0:8, :BLK]
         two = both[8:16, BLK:]
-        slots_ref[pl.ds(route_ref[1, 2 * p], NF), :] = one[:NF] + one[NF:]
-        slots_ref[pl.ds(route_ref[1, 2 * p + 1], NF), :] = two[:NF] + two[NF:]
-
-    @pl.loop(0, EPD // 2, step=UNROLL)
-    def _(start):
-        for k in range(UNROLL):
-            pair(start + k)
+        slots_ref[pl.ds(route_ref[1, e], NF), :] = one[:NF] + one[NF:]
+        slots_ref[pl.ds(route_ref[1, e + 1], NF), :] = two[:NF] + two[NF:]
+
+    def pairs(ref, first, unroll):
+        @pl.loop(0, ref.shape[0], step=unroll)
+        def _(start):
+            for k in range(unroll):
+                pair(ref, start + k, first)
+
+    pairs(halves_ref, 0, UNROLL)
+    pairs(later_ref, halves_ref.shape[0], later_ref.shape[0])
 
 
 def aloft_kernel(
@@ -185,13 +225,12 @@
     def _():
         keep_ref[...] = inside(meta_ref).astype(jnp.float32)
 
-    for k in range(NF):
-        level = group * NF + k
-        field = extended(
-            x_ref[k], top_ref[k], bottom_ref[k], left_ref[...], right_ref[...], level
-        )
-        field = evolve(field, keep_ref[...], diffusion_ref[0, level], courant_ref[0, level], meta_ref[4])
-        out_ref[k] = field[:CX, :CY]
+    fields = extended_group(
+        meta_ref, (diffusion_ref, courant_ref), x_ref, top_ref, bottom_ref, left_ref, right_ref,
+        keep_ref, group * NF,
+    )
+    for k, field in enumerate(fields):
+        out_ref[k] = field
 
 
 def finish_kernel(slots_ref, surface_ref, coef_ref, aloft_ref, state_ref, remapped_ref):
@@ -227,6 +266,9 @@
     vmem = pl.BlockSpec(memory_space=pltpu.VMEM)
     anywhere = pl.BlockSpec(memory_space=pl.ANY)
 
+    def in_hbm(value):
+        return pltpu.with_memory_space_constraint(value, pltpu.HBM)
+
     def limit(mib):
         return pltpu.CompilerParams(vmem_limit_bytes=mib << 20)
 
@@ -245,33 +287,24 @@
 
     with jax.named_scope("prepare"):
         centre = jax.ShapeDtypeStruct((CX, BLK), jnp.float32)
-        halves, route, label, left, right = pl.pallas_call(
+        halves, left, right = pl.pallas_call(
             prepare_kernel,
-            in_specs=[anywhere, anywhere, vmem, vmem, vmem, anywhere],
-            out_specs=[vmem] * 5,
+            in_specs=[anywhere] * 3,
+            out_specs=[vmem] * 3,
             out_shape=(
-                pltpu.VMEM((EPD // 2, 2 * BLK, 2 * BLK), jnp.bfloat16),
-                jax.ShapeDtypeStruct((2, EPD), jnp.int32),
-                jax.ShapeDtypeStruct((peers, BLK), jnp.float32),
+                pltpu.VMEM(((N_CHUNKS - LATER) * CHUNK // 2, 2 * BLK, 2 * BLK), jnp.bfloat16),
                 centre,
                 centre,
             ),
             scratch_shapes=[
-                pltpu.VMEM((EPD, BLK, BLK), jnp.float32),
+                pltpu.VMEM(((N_CHUNKS - LATER) * CHUNK, BLK, BLK), jnp.float32),
                 pltpu.VMEM((LEV, CX, CY), jnp.float32),
-                pltpu.SemaphoreType.DMA((N_CHUNKS,)),
+                pltpu.SemaphoreType.DMA((N_CHUNKS - LATER,)),
                 pltpu.SemaphoreType.DMA,
             ],
-            compiler_params=limit(18),
+            compiler_params=limit(16),
             name="prepare",
-        )(
-            pltpu.with_memory_space_constraint(remap_weight[0], pltpu.HBM),
-            pltpu.with_memory_space_constraint(x, pltpu.HBM),
-            src_block,
-            dest_peer.reshape(1, EPD),
-            dest_block,
-            meta,
-        )
+        )(in_hbm(remap_weight[0]), in_hbm(x), meta)
 
     with jax.named_scope("halo"):
         side = jax.ShapeDtypeStruct((ROWS, BLK), jnp.float32)
@@ -280,6 +313,23 @@
         )(top, bottom, left, right)
         from_right = lax.ppermute(left, "gy", ring("gy", -1))
         from_left = lax.ppermute(right, "gy", ring("gy", 1))
+
+    later, route, label = pl.pallas_call(
+        route_kernel,
+        in_specs=[anywhere, vmem, vmem, vmem, anywhere],
+        out_specs=[vmem] * 3,
+        out_shape=(
+            pltpu.VMEM((LATER * CHUNK // 2, 2 * BLK, 2 * BLK), jnp.bfloat16),
+            jax.ShapeDtypeStruct((2, EPD), jnp.int32),
+            jax.ShapeDtypeStruct((peers, BLK), jnp.float32),
+        ),
+        scratch_shapes=[
+            pltpu.VMEM((LATER * CHUNK, BLK, BLK), jnp.float32),
+            pltpu.SemaphoreType.DMA((LATER,)),
+        ],
+        compiler_params=limit(6),
+        name="route",
+    )(in_hbm(remap_weight[0]), src_block, dest_peer.reshape(1, EPD), dest_block, left)
 
     tile = pl.BlockSpec((NF, CX, CY), lambda i: (0, 0, 0))
     edge = pl.BlockSpec((NF, HALO, CY), lambda i: (0, 0, 0))
@@ -289,7 +339,7 @@
         grid=(1,),
         in_specs=[
             smem, smem, smem, smem, tile, edge, edge, whole, whole,
-            pl.BlockSpec((peers, BLK), lambda i: (0, 0)), vmem,
+            pl.BlockSpec((peers, BLK), lambda i: (0, 0)), vmem, vmem,
         ],
         out_specs=[pl.BlockSpec((rows_out, BLK), lambda i: (0, 0)), tile],
         out_shape=(
@@ -303,7 +353,8 @@
         compiler_params=limit(6),
         name="surface",
     )(
-        meta, diffusion, courant, route, x, top, bottom, from_left, from_right, label, halves
+        meta, diffusion, courant, route, x, top, bottom, from_left, from_right, label, halves,
+        later,
     )
 
     tile_up = pl.BlockSpec((NF, CX, CY), lambda i: (i + 1, 0, 0))

time: 75.5 us -> 68.8 us (0.911)
  Pallas kernels: 22.7 us -> 17 us
  local copies, waits for them, and re-layouts: 3.2 us -> 1.13 us
  waiting for transfers between devices: 21.4 us -> 23.2 us
    pallas_call x1, Pallas kernels: 7.23 us -> 3.7 us  [body(): pl.pallas_call(surface_kernel, grid=(1,), in_specs=[smem, smem, smem, sme...]
    all_to_all x1, waiting for transfers between devices: 18.1 us -> 21 us  [body(): lax.all_to_all(outgoing.reshape(peers, ROWS_PER_PEER, 1, BLK), ('gx', 'gy...]
    pallas_call x1, Pallas kernels: 7.15 us -> 4.2 us  [body(): pl.pallas_call(aloft_kernel, grid=(LEV // NF - 1,), in_specs=[smem, smem,...]
    ppermute x1, starting transfers between devices: 0.01 us -> 2.54 us  [body(): top = lax.ppermute(x[:, CX - HALO:], 'gx', ring('gx', 1))]
    ppermute x1, starting transfers between devices: 6.48 us -> 4.03 us  [body(): bottom = lax.ppermute(x[:, :HALO], 'gx', ring('gx', -1))]
    unnamed x14, local copies, waits for them, and re-layouts: 2.06 us -> 0.04 us
    ppermute x1, starting transfers between devices: 3.57 us -> 2.13 us  [body(): outgoing = lax.ppermute(outgoing, 'sec', ring('sec', 1))]
    ppermute x1, waiting for transfers between devices: 1.21 us -> 0.01 us  [body(): from_left = lax.ppermute(right, 'gy', ring('gy', 1))]
  transfers between devices with their start and end apart: 6 -> 6, of which waited for: 3 -> 2; matrix products, arithmetic and copies ran while one was open for 0% -> 0% of each run, Pallas kernels for 19% -> 18%
where the time goes in v4:
time: 68.8 us; the launch traced here: 68 us
  starting transfers between devices  25.9 us (38%)
  waiting for transfers between devices  23.2 us (34%)
  Pallas kernels  17 us (25%)
  local copies, waits for them, and re-layouts  1.13 us (2%)
  between operations  0.78 us (1%)
    all_to_all x1, waiting for transfers between devices, body(): lax.all_to_all(outgoing.reshape(peers, ROWS_PER_PEER, 1, BLK), ('gx', 'gy...  21 us
    all_to_all x1, starting transfers between devices, body(): lax.all_to_all(outgoing.reshape(peers, ROWS_PER_PEER, 1, BLK), ('gx', 'gy...  12.1 us
    pallas_call x1, Pallas kernels, body(): pl.pallas_call(prepare_kernel, in_specs=[anywhere] * 3, out_specs=[vmem]...  5.55 us
    pallas_call x1, Pallas kernels, body(): pl.pallas_call(aloft_kernel, grid=(LEV // NF - 1,), in_specs=[smem, smem,...  4.2 us
    ppermute x1, starting transfers between devices, body(): bottom = lax.ppermute(x[:, :HALO], 'gx', ring('gx', -1))  4.03 us
    ppermute x1, starting transfers between devices, body(): from_right = lax.ppermute(left, 'gy', ring('gy', -1))  3.81 us
    pallas_call x1, Pallas kernels, body(): pl.pallas_call(surface_kernel, grid=(1,), in_specs=[smem, smem, smem, sme...  3.7 us
    ppermute x1, starting transfers between devices, body(): top = lax.ppermute(x[:, CX - HALO:], 'gx', ring('gx', 1))  2.54 us
  transfers between devices with their start and end apart: 6, of which 2 were waited for; matrix products, arithmetic and copies ran while one was open for 0% of the time, Pallas kernels for 18%

profile of v4, /device:TPU:1, one launch (start us, length us, event | category | flops | bytes accessed | tf_op | source)
XLA Modules:
  0.0 68.0 jit_solution(7980604083090287320)
XLA Ops:
  0.6 0.0 copy-start.4
  0.6 0.0 copy-start.5
  0.7 0.0 copy-start.6
  0.7 1.0 %fusion = (f32[16,8,256]{2,1,0:T(8,128)S(1)}, f32[16,8,256]{2,1,0:T(8,128)S(1)}) fusion(f32[16,48,256]{2,1,0:T(8,128)} %bitcast.11), kind=kLoop, calls=%fused_computation | loop fusion | bytes 524288 | tf_op jit(solution)/shard_map/halo/slice | solution.py:286
  1.7 2.5 %collective-permute-start = (f32[16,8,256]{2,1,0:T(8,128)S(1)}, f32[16,8,256]{2,1,0:T(8,128)S(1)}, u32[]{:S(2)}, u32[]{:S(2)}) collective-permute-start(f32[16,8,256]{2,1,0:T(8,128)S(1)} %get-tuple-element.27), channel_id=1, source_target_pairs={{0,16},{16,32},{32,48},{48,64},{64,80},{80,96},{96,112},{112,0},{1... | collective-permute-start | bytes 393224 | tf_op jit(solution)/shard_map/halo/ppermute | solution.py:285
  4.2 4.0 %collective-permute-start.1 = (f32[16,8,256]{2,1,0:T(8,128)S(1)}, f32[16,8,256]{2,1,0:T(8,128)S(1)}, u32[]{:S(2)}, u32[]{:S(2)}) collective-permute-start(f32[16,8,256]{2,1,0:T(8,128)S(1)} %get-tuple-element.26), channel_id=1, source_target_pairs={{0,112},{16,0},{32,16},{48,32},{64,48},{80,64},{96,80},{112,96},{1... | collective-permute-start | bytes 393224 | tf_op jit(solution)/shard_map/halo/ppermute | solution.py:286
  8.2 0.1 stack.15.meta_ref
  8.3 5.6 %prepare.1 = (bf16[72,256,256]{2,1,0:T(8,128)(2,1)S(1)}, f32[48,128]{1,0:T(8,128)S(1)}, f32[48,128]{1,0:T(8,128)S(1)}) custom-call(f32[192,128,128]{2,1,0:T(8,128)} %bitcast.18, f32[16,48,256]{2,1,0:T(8,128)} %bitcast.12, s32[5]{0:T(128)S(1)} %stack.15.meta_ref), custom_call_target="tpu_custom_call" | custom-call | tf_op jit(solution)/shard_map/prepare/prepare/pallas_call | solution.py:290
  13.9 0.0 copy-start
  13.9 0.0 copy-start.2
  13.9 0.0 copy-start.3
  13.9 0.0 collective-permute-done.top_ref
  13.9 0.0 collective-permute-done.1.bottom_ref
  13.9 0.1 pack.1
  14.1 1.3 %collective-permute-start.2 = (f32[64,128]{1,0:T(8,128)S(1)}, f32[64,128]{1,0:T(8,128)S(1)}, u32[]{:S(2)}, u32[]{:S(2)}) collective-permute-start(f32[64,128]{1,0:T(8,128)S(1)} %get-tuple-element.18), channel_id=1, source_target_pairs={{0,1},{1,2},{2,3},{3,4},{4,5},{5,6},{6,7},{7,8},{8,9},{9,10},{10,1... | collective-permute-start | bytes 98312 | tf_op jit(solution)/shard_map/halo/ppermute | solution.py:315
  15.4 3.8 %collective-permute-start.3 = (f32[64,128]{1,0:T(8,128)S(1)}, f32[64,128]{1,0:T(8,128)S(1)}, u32[]{:S(2)}, u32[]{:S(2)}) collective-permute-start(f32[64,128]{1,0:T(8,128)S(1)} %get-tuple-element.16.after_ref), channel_id=1, source_target_pairs={{0,15},{1,0},{2,1},{3,2},{4,3},{5,4},{6,5},{7,6},{8,7},{9,8},{10,9... | collective-permute-start | bytes 98312 | tf_op jit(solution)/shard_map/halo/ppermute | solution.py:314
  19.2 0.0 copy-done.4
  19.2 0.0 copy-done.5
  19.2 0.0 copy-done.6
  19.2 2.3 %route.1 = (bf16[24,256,256]{2,1,0:T(8,128)(2,1)S(1)}, s32[2,192]{1,0:T(2,128)S(1)}, f32[128,128]{1,0:T(8,128)S(1)}) custom-call(f32[192,128,128]{2,1,0:T(8,128)} %bitcast.19, s32[1,192]{1,0:T(1,128)S(1)} %copy-done.4, s32[1,192]{1,0:T(1,128)S(1)} %bitcast.17, s32[1,192]{1,0:T(1,128)S(1)} %copy-done.6, f32[64,128]{1,0:T(8,128)S(1)} %get-tuple-element.16.after_ref), custom_call_target="tpu_custom_call" | custom-call | tf_op jit(solution)/shard_map/route/pallas_call | solution.py:317
  21.5 0.0 copy-start.1
  21.5 0.0 collective-permute-done.2.left_ref
  21.5 0.0 collective-permute-done.3.right_ref
  21.5 0.0 copy-done
  21.5 3.7 %surface.1 = (f32[1664,128]{1,0:T(8,128)S(1)}, f32[4,48,256]{2,1,0:T(8,128)S(1)}) custom-call(s32[5]{0:T(128)S(1)} %stack.15.meta_ref, f32[1,16]{1,0:T(1,128)S(1)} %copy-done.2, f32[1,16]{1,0:T(1,128)S(1)} %copy-done.3, s32[2,192]{1,0:T(2,128)S(1)} %get-tuple-element.17.route_ref, f32[16,48,256]{2,1,0:T(8,128)S(1)} %bitcast.13, ...), custom_call_target="tpu_custom_call" | custom-call | tf_op jit(solution)/shard_map/surface/pallas_call | solution.py:337
  25.2 2.1 %collective-permute-start.4 = (f32[1664,128]{1,0:T(8,128)S(1)}, f32[1664,128]{1,0:T(8,128)}, u32[]{:S(2)}, u32[]{:S(2)}) collective-permute-start(f32[1664,128]{1,0:T(8,128)S(1)} %get-tuple-element.22), channel_id=1, source_target_pairs={{0,128},{128,0},{1,129},{129,1},{2,130},{130,2},{3,131},{131,3},{4... | collective-permute-start | bytes 2555912 | tf_op jit(solution)/shard_map/ppermute | solution.py:373
  27.4 2.1 %collective-permute-done.4 = f32[1664,128]{1,0:T(8,128)} collective-permute-done((f32[1664,128]{1,0:T(8,128)S(1)}, f32[1664,128]{1,0:T(8,128)}, u32[]{:S(2)}, u32[]{:S(2)}) %collective-permute-start.4) | collective-permute-done | bytes 852000 | tf_op jit(solution)/shard_map/ppermute | solution.py:373
  29.5 12.1 %all-to-all-start = ((f32[128,13,1,128]{3,2,1,0:T(1,128)}), f32[128,13,1,128]{3,2,1,0:T(1,128)S(1)}, u32[]{:S(2)}, u32[]{:S(2)}) async-start(f32[128,13,1,128]{3,2,1,0:T(1,128)} %bitcast.6), calls=%async_computation | async-start | bytes 1703936 | tf_op jit(solution)/shard_map/all_to_all | solution.py:374
  41.6 4.2 %aloft.1.aloft_ref = f32[16,48,256]{2,1,0:T(8,128)} custom-call(s32[5]{0:T(128)S(1)} %stack.15.meta_ref, f32[1,16]{1,0:T(1,128)S(1)} %copy-done.2, f32[1,16]{1,0:T(1,128)S(1)} %copy-done.3, f32[16,48,256]{2,1,0:T(8,128)S(1)} %bitcast.14, f32[16,8,256]{2,1,0:T(8,128)S(1)} %collective-permute-done.top_ref, ...), custom_call_target="tpu_custom_call" | custom-call | tf_op jit(solution)/shard_map/aloft/pallas_call | solution.py:362
  45.8 21.0 %all-to-all-done = f32[128,13,1,128]{3,2,1,0:T(1,128)S(1)} async-done(((f32[128,13,1,128]{3,2,1,0:T(1,128)}), f32[128,13,1,128]{3,2,1,0:T(1,128)S(1)}, u32[]{:S(2)}, u32[]{:S(2)}) %all-to-all-start) | async-done | bytes 852000 | tf_op jit(solution)/shard_map/all_to_all | solution.py:374
  66.8 0.0 copy-done.1
  66.8 1.2 %finish.1 = (f32[16,48,256]{2,1,0:T(8,128)}, f32[4,48,256]{2,1,0:T(8,128)}) custom-call(f32[1664,128]{1,0:T(8,128)S(1)} %bitcast.15, f32[4,48,256]{2,1,0:T(8,128)S(1)} %get-tuple-element.23.surface_ref, f32[48,256]{1,0:T(8,128)S(1)} %bitcast.16, f32[16,48,256]{2,1,0:T(8,128)} %aloft.1.aloft_ref), custom_call_target="tpu_custom_call", output_to_operand_aliasing={{0}: (3, {})} | custom-call | tf_op jit(solution)/shard_map/finish/pallas_call | solution.py:379
  (2 shorter events, 0.0 us)
Async XLA Ops:
  0.6 18.5 %copy-start.4 = (s32[1,192]{1,0:T(1,128)S(1)}, s32[1,192]{1,0:T(1,128)}, u32[]{:S(2)}) copy-start(s32[1,192]{1,0:T(1,128)} %source_ref.1) | copy-start | bytes 2308
  0.6 18.5 %copy-start.5 = (s32[1,192,1]{1,2,0:T(1,128)S(1)}, s32[1,192,1]{1,2,0:T(1,128)}, u32[]{:S(2)}) copy-start(s32[1,192,1]{1,2,0:T(1,128)} %param.13) | copy-start | bytes 2308
  0.7 18.5 %copy-start.6 = (s32[1,192]{1,0:T(1,128)S(1)}, s32[1,192]{1,0:T(1,128)}, u32[]{:S(2)}) copy-start(s32[1,192]{1,0:T(1,128)} %block_ref.1) | copy-start | bytes 2308
  1.7 12.3 %collective-permute-start = (f32[16,8,256]{2,1,0:T(8,128)S(1)}, f32[16,8,256]{2,1,0:T(8,128)S(1)}, u32[]{:S(2)}, u32[]{:S(2)}) collective-permute-start(f32[16,8,256]{2,1,0:T(8,128)S(1)} %get-tuple-element.27), channel_id=1, source_target_pairs={{0,16},{16,32},{32,48},{48,64},{64,80},{80,96},{96,112},{112,0},{1... | collective-permute-start | bytes 393224 | tf_op jit(solution)/shard_map/halo/ppermute | solution.py:285
  4.2 9.7 %collective-permute-start.1 = (f32[16,8,256]{2,1,0:T(8,128)S(1)}, f32[16,8,256]{2,1,0:T(8,128)S(1)}, u32[]{:S(2)}, u32[]{:S(2)}) collective-permute-start(f32[16,8,256]{2,1,0:T(8,128)S(1)} %get-tuple-element.26), channel_id=1, source_target_pairs={{0,112},{16,0},{32,16},{48,32},{64,48},{80,64},{96,80},{112,96},{1... | collective-permute-start | bytes 393224 | tf_op jit(solution)/shard_map/halo/ppermute | solution.py:286
  13.9 7.6 %copy-start = (f32[1,16,48,256]{3,2,1,0:T(8,128)S(1)}, f32[1,16,48,256]{3,2,1,0:T(8,128)}, u32[]{:S(2)}) copy-start(f32[1,16,48,256]{3,2,1,0:T(8,128)} %param.8) | copy-start | bytes 2359300
  13.9 7.6 %copy-start.2 = (f32[1,16]{1,0:T(1,128)S(1)}, f32[1,16]{1,0:T(1,128)}, u32[]{:S(2)}) copy-start(f32[1,16]{1,0:T(1,128)} %diffusion_ref.3) | copy-start | bytes 196
  13.9 7.6 %copy-start.3 = (f32[1,16]{1,0:T(1,128)S(1)}, f32[1,16]{1,0:T(1,128)}, u32[]{:S(2)}) copy-start(f32[1,16]{1,0:T(1,128)} %courant_ref.3) | copy-start | bytes 196
  14.1 7.4 %collective-permute-start.2 = (f32[64,128]{1,0:T(8,128)S(1)}, f32[64,128]{1,0:T(8,128)S(1)}, u32[]{:S(2)}, u32[]{:S(2)}) collective-permute-start(f32[64,128]{1,0:T(8,128)S(1)} %get-tuple-element.18), channel_id=1, source_target_pairs={{0,1},{1,2},{2,3},{3,4},{4,5},{5,6},{6,7},{7,8},{8,9},{9,10},{10,1... | collective-permute-start | bytes 98312 | tf_op jit(solution)/shard_map/halo/ppermute | solution.py:315
  15.4 6.1 %collective-permute-start.3 = (f32[64,128]{1,0:T(8,128)S(1)}, f32[64,128]{1,0:T(8,128)S(1)}, u32[]{:S(2)}, u32[]{:S(2)}) collective-permute-start(f32[64,128]{1,0:T(8,128)S(1)} %get-tuple-element.16.after_ref), channel_id=1, source_target_pairs={{0,15},{1,0},{2,1},{3,2},{4,3},{5,4},{6,5},{7,6},{8,7},{9,8},{10,9... | collective-permute-start | bytes 98312 | tf_op jit(solution)/shard_map/halo/ppermute | solution.py:314
  21.5 45.3 %copy-start.1 = (f32[1,48,256]{2,1,0:T(8,128)S(1)}, f32[1,48,256]{2,1,0:T(8,128)}, u32[]{:S(2)}) copy-start(f32[1,48,256]{2,1,0:T(8,128)} %param.11) | copy-start | bytes 147460
  25.2 4.3 %collective-permute-start.4 = (f32[1664,128]{1,0:T(8,128)S(1)}, f32[1664,128]{1,0:T(8,128)}, u32[]{:S(2)}, u32[]{:S(2)}) collective-permute-start(f32[1664,128]{1,0:T(8,128)S(1)} %get-tuple-element.22), channel_id=1, source_target_pairs={{0,128},{128,0},{1,129},{129,1},{2,130},{130,2},{3,131},{131,3},{4... | collective-permute-start | bytes 2555912 | tf_op jit(solution)/shard_map/ppermute | solution.py:373
  29.5 37.3 %all-to-all-start = ((f32[128,13,1,128]{3,2,1,0:T(1,128)}), f32[128,13,1,128]{3,2,1,0:T(1,128)S(1)}, u32[]{:S(2)}, u32[]{:S(2)}) async-start(f32[128,13,1,128]{3,2,1,0:T(1,128)} %bitcast.6), calls=%async_computation | async-start | bytes 1703936 | tf_op jit(solution)/shard_map/all_to_all | solution.py:374

commit v5 on v4

--- a/solution.py
+++ b/solution.py
@@ -21,8 +21,8 @@
 CHUNK = 16
 N_CHUNKS = EPD // CHUNK
 ROWS_PER_PEER = CAP * NF + 1
-UNROLL = 36
-LATER = 3
+UNROLL = 28
+LATER = 5
 DEPTH = 4
 
 
@@ -111,9 +111,10 @@
 ):
     del meta_ref
     tile = pltpu.make_async_copy(x_ref, x_buf, x_sem)
-    tile.start()
     begin, finish = split_parts(w_ref, w_buf, w_sems, halves_ref, 0)
     begin()
+    tile.start()
+    finish()
     tile.wait()
     lane = lax.broadcasted_iota(jnp.int32, (CX, BLK), 1) // HALO
     left = jnp.zeros((CX, BLK), jnp.float32)
@@ -122,7 +123,6 @@
         left, right = packed(x_buf[level], left, right, lane, level)
     left_ref[...] = left
     right_ref[...] = right
-    finish()
 
 
 def route_kernel(
@@ -233,8 +233,7 @@
         out_ref[k] = field
 
 
-def finish_kernel(slots_ref, surface_ref, coef_ref, aloft_ref, state_ref, remapped_ref):
-    del aloft_ref
+def combine_kernel(slots_ref, total_ref):
     peers = slots_ref.shape[0] // ROWS_PER_PEER
     labels = slots_ref[pl.ds(ROWS_PER_PEER - 1, peers, stride=ROWS_PER_PEER), :].T
     row = lax.broadcasted_iota(jnp.int32, (BPD, peers), 0)
@@ -249,7 +248,13 @@
             low = (data - high.astype(jnp.float32)).astype(jnp.bfloat16)
             total += lax.dot_general(chosen[k], high, dims, preferred_element_type=jnp.float32)
             total += lax.dot_general(chosen[k], low, dims, preferred_element_type=jnp.float32)
-        total = jnp.concatenate([total[:CX], total[CX:]], axis=1)
+        total_ref[level] = jnp.concatenate([total[:CX], total[CX:]], axis=1)
+
+
+def finish_kernel(total_ref, surface_ref, coef_ref, aloft_ref, state_ref, remapped_ref):
+    del aloft_ref
+    for level in range(NF):
+        total = total_ref[level]
         remapped_ref[level] = total
         surface = surface_ref[level]
         state_ref[level] = surface + coef_ref[...] * jnp.tanh(total - surface)
@@ -370,17 +375,24 @@
         name="aloft",
     )(meta, diffusion, courant, x, top, bottom, from_left, from_right)
 
-    outgoing = lax.ppermute(outgoing, "sec", ring("sec", 1))
     incoming = lax.all_to_all(
         outgoing.reshape(peers, ROWS_PER_PEER, 1, BLK), ("gx", "gy"), split_axis=0, concat_axis=0, tiled=True
     )
     incoming = incoming.reshape(rows_out, BLK)
+    incoming, aloft = lax.optimization_barrier((incoming, aloft))
+    total = pl.pallas_call(
+        combine_kernel,
+        out_shape=jax.ShapeDtypeStruct((NF, CX, CY), jnp.float32),
+        compiler_params=limit(3),
+        name="combine",
+    )(incoming)
+    total = lax.ppermute(total, "sec", ring("sec", 1))
 
     new_state, remapped = pl.pallas_call(
         finish_kernel,
         grid=(1,),
         in_specs=[
-            pl.BlockSpec((rows_out, BLK), lambda i: (0, 0)),
+            tile,
             tile,
             pl.BlockSpec((CX, CY), lambda i: (0, 0)),
             pl.BlockSpec(memory_space=pl.ANY),
@@ -393,7 +405,7 @@
         input_output_aliases={3: 0},
         compiler_params=limit(5),
         name="finish",
-    )(incoming, surface, exchange_coef[0], aloft)
+    )(total, surface, exchange_coef[0], aloft)
     return (new_state[None], remapped[None])
 
 

time: 68.8 us -> 66.5 us (0.967)
  waiting for transfers between devices: 23.2 us -> 19.4 us
  starting transfers between devices: 25.9 us -> 27.5 us
    ppermute x1, starting transfers between devices: 2.13 us -> 5.76 us  [body(): total = lax.ppermute(total, 'sec', ring('sec', 1))]
    all_to_all x1, waiting for transfers between devices: 21 us -> 18.3 us  [body(): lax.all_to_all(outgoing.reshape(peers, ROWS_PER_PEER, 1, BLK), ('gx', 'gy...]
    all_to_all x1, starting transfers between devices: 12.1 us -> 10.1 us  [body(): lax.all_to_all(outgoing.reshape(peers, ROWS_PER_PEER, 1, BLK), ('gx', 'gy...]
    pallas_call x1, Pallas kernels: 5.55 us -> 4.3 us  [body(): pl.pallas_call(prepare_kernel, in_specs=[anywhere] * 3, out_specs=[vmem]...]
    ppermute x1, waiting for transfers between devices: 2.14 us -> 1.07 us  [body(): total = lax.ppermute(total, 'sec', ring('sec', 1))]
    pallas_call x1, Pallas kernels: 3.7 us -> 4.62 us  [body(): pl.pallas_call(surface_kernel, grid=(1,), in_specs=[smem, smem, smem, sme...]
    pallas_call x1, Pallas kernels: 2.28 us -> 3.1 us  [body(): pl.pallas_call(route_kernel, in_specs=[anywhere, vmem, vmem, vmem, anywhe...]
where the time goes in v5:
time: 66.5 us; the launch traced here: 66.3 us
  starting transfers between devices  27.5 us (41%)
  waiting for transfers between devices  19.4 us (29%)
  Pallas kernels  17.5 us (26%)
  local copies, waits for them, and re-layouts  1.13 us (2%)
  between operations  0.78 us (1%)
    all_to_all x1, waiting for transfers between devices, body(): lax.all_to_all(outgoing.reshape(peers, ROWS_PER_PEER, 1, BLK), ('gx', 'gy...  18.3 us
    all_to_all x1, starting transfers between devices, body(): lax.all_to_all(outgoing.reshape(peers, ROWS_PER_PEER, 1, BLK), ('gx', 'gy...  10.1 us
    ppermute x1, starting transfers between devices, body(): total = lax.ppermute(total, 'sec', ring('sec', 1))  5.76 us
    pallas_call x1, Pallas kernels, body(): pl.pallas_call(surface_kernel, grid=(1,), in_specs=[smem, smem, smem, sme...  4.62 us
    pallas_call x1, Pallas kernels, body(): pl.pallas_call(prepare_kernel, in_specs=[anywhere] * 3, out_specs=[vmem]...  4.3 us
    pallas_call x1, Pallas kernels, body(): pl.pallas_call(aloft_kernel, grid=(LEV // NF - 1,), in_specs=[smem, smem,...  4.2 us
    ppermute x1, starting transfers between devices, body(): bottom = lax.ppermute(x[:, :HALO], 'gx', ring('gx', -1))  4.03 us
    ppermute x1, starting transfers between devices, body(): from_right = lax.ppermute(left, 'gy', ring('gy', -1))  3.81 us
  transfers between devices with their start and end apart: 6, of which 2 were waited for; matrix products, arithmetic and copies ran while one was open for 0% of the time, Pallas kernels for 18%

profile of v5, /device:TPU:1, one launch (start us, length us, event | category | flops | bytes accessed | tf_op | source)
XLA Modules:
  0.0 66.3 jit_solution(7469310863631380396)
XLA Ops:
  0.6 0.0 copy-start.4
  0.6 0.0 copy-start.5
  0.7 0.0 copy-start.6
  0.7 1.0 %fusion = (f32[16,8,256]{2,1,0:T(8,128)S(1)}, f32[16,8,256]{2,1,0:T(8,128)S(1)}) fusion(f32[16,48,256]{2,1,0:T(8,128)} %bitcast.11), kind=kLoop, calls=%fused_computation | loop fusion | bytes 524288 | tf_op jit(solution)/shard_map/halo/slice | solution.py:291
  1.7 2.5 %collective-permute-start = (f32[16,8,256]{2,1,0:T(8,128)S(1)}, f32[16,8,256]{2,1,0:T(8,128)S(1)}, u32[]{:S(2)}, u32[]{:S(2)}) collective-permute-start(f32[16,8,256]{2,1,0:T(8,128)S(1)} %get-tuple-element.31), channel_id=1, source_target_pairs={{0,16},{16,32},{32,48},{48,64},{64,80},{80,96},{96,112},{112,0},{1... | collective-permute-start | bytes 393224 | tf_op jit(solution)/shard_map/halo/ppermute | solution.py:290
  4.2 4.0 %collective-permute-start.1 = (f32[16,8,256]{2,1,0:T(8,128)S(1)}, f32[16,8,256]{2,1,0:T(8,128)S(1)}, u32[]{:S(2)}, u32[]{:S(2)}) collective-permute-start(f32[16,8,256]{2,1,0:T(8,128)S(1)} %get-tuple-element.30), channel_id=1, source_target_pairs={{0,112},{16,0},{32,16},{48,32},{64,48},{80,64},{96,80},{112,96},{1... | collective-permute-start | bytes 393224 | tf_op jit(solution)/shard_map/halo/ppermute | solution.py:291
  8.2 0.1 stack.15.meta_ref
  8.3 4.3 %prepare.1 = (bf16[56,256,256]{2,1,0:T(8,128)(2,1)S(1)}, f32[48,128]{1,0:T(8,128)S(1)}, f32[48,128]{1,0:T(8,128)S(1)}) custom-call(f32[192,128,128]{2,1,0:T(8,128)} %bitcast.18, f32[16,48,256]{2,1,0:T(8,128)} %bitcast.12, s32[5]{0:T(128)S(1)} %stack.15.meta_ref), custom_call_target="tpu_custom_call" | custom-call | tf_op jit(solution)/shard_map/prepare/prepare/pallas_call | solution.py:295
  12.6 0.0 copy-start
  12.6 0.0 copy-start.2
  12.7 0.0 copy-start.3
  12.7 0.0 collective-permute-done.top_ref
  12.7 0.0 collective-permute-done.1.bottom_ref
  12.7 0.1 pack.1
  12.8 1.3 %collective-permute-start.2 = (f32[64,128]{1,0:T(8,128)S(1)}, f32[64,128]{1,0:T(8,128)S(1)}, u32[]{:S(2)}, u32[]{:S(2)}) collective-permute-start(f32[64,128]{1,0:T(8,128)S(1)} %get-tuple-element.20), channel_id=1, source_target_pairs={{0,1},{1,2},{2,3},{3,4},{4,5},{5,6},{6,7},{7,8},{8,9},{9,10},{10,1... | collective-permute-start | bytes 98312 | tf_op jit(solution)/shard_map/halo/ppermute | solution.py:320
  14.1 3.8 %collective-permute-start.3 = (f32[64,128]{1,0:T(8,128)S(1)}, f32[64,128]{1,0:T(8,128)S(1)}, u32[]{:S(2)}, u32[]{:S(2)}) collective-permute-start(f32[64,128]{1,0:T(8,128)S(1)} %get-tuple-element.18.after_ref), channel_id=1, source_target_pairs={{0,15},{1,0},{2,1},{3,2},{4,3},{5,4},{6,5},{7,6},{8,7},{9,8},{10,9... | collective-permute-start | bytes 98312 | tf_op jit(solution)/shard_map/halo/ppermute | solution.py:319
  17.9 0.0 copy-done.4
  17.9 3.1 %route.1 = (bf16[40,256,256]{2,1,0:T(8,128)(2,1)S(1)}, s32[2,192]{1,0:T(2,128)S(1)}, f32[128,128]{1,0:T(8,128)S(1)}) custom-call(f32[192,128,128]{2,1,0:T(8,128)} %bitcast.19, s32[1,192]{1,0:T(1,128)S(1)} %copy-done.4, s32[1,192]{1,0:T(1,128)S(1)} %bitcast.17, s32[1,192]{1,0:T(1,128)S(1)} %copy-done.6, f32[64,128]{1,0:T(8,128)S(1)} %get-tuple-element.18.after_ref), custom_call_target="tpu_custom_call" | custom-call | tf_op jit(solution)/shard_map/route/pallas_call | solution.py:322
  21.0 0.0 collective-permute-done.2.left_ref
  21.0 0.0 collective-permute-done.3.right_ref
  21.1 0.0 copy-done
  21.1 0.0 copy-done.2
  21.1 0.0 copy-done.3
  21.1 0.0 copy-start.1
  21.1 4.6 %surface.1 = (f32[1664,128]{1,0:T(8,128)}, f32[4,48,256]{2,1,0:T(8,128)S(1)}) custom-call(s32[5]{0:T(128)S(1)} %stack.15.meta_ref, f32[1,16]{1,0:T(1,128)S(1)} %copy-done.2, f32[1,16]{1,0:T(1,128)S(1)} %copy-done.3, s32[2,192]{1,0:T(2,128)S(1)} %get-tuple-element.19.route_ref, f32[16,48,256]{2,1,0:T(8,128)S(1)} %bitcast.13, ...), custom_call_target="tpu_custom_call" | custom-call | tf_op jit(solution)/shard_map/surface/pallas_call | solution.py:342
  25.7 10.1 %all-to-all-start = ((f32[128,13,1,128]{3,2,1,0:T(1,128)}), f32[128,13,1,128]{3,2,1,0:T(1,128)S(1)}, u32[]{:S(2)}, u32[]{:S(2)}) async-start(f32[128,13,1,128]{3,2,1,0:T(1,128)} %bitcast.6), calls=%async_computation | async-start | bytes 1703936 | tf_op jit(solution)/shard_map/all_to_all | solution.py:378
  35.8 4.2 %aloft.1.aloft_ref = f32[16,48,256]{2,1,0:T(8,128)} custom-call(s32[5]{0:T(128)S(1)} %stack.15.meta_ref, f32[1,16]{1,0:T(1,128)S(1)} %copy-done.2, f32[1,16]{1,0:T(1,128)S(1)} %copy-done.3, f32[16,48,256]{2,1,0:T(8,128)S(1)} %bitcast.14, f32[16,8,256]{2,1,0:T(8,128)S(1)} %collective-permute-done.top_ref, ...), custom_call_target="tpu_custom_call" | custom-call | tf_op jit(solution)/shard_map/aloft/pallas_call | solution.py:367
  40.0 18.3 %all-to-all-done = f32[128,13,1,128]{3,2,1,0:T(1,128)S(1)} async-done(((f32[128,13,1,128]{3,2,1,0:T(1,128)}), f32[128,13,1,128]{3,2,1,0:T(1,128)S(1)}, u32[]{:S(2)}, u32[]{:S(2)}) %all-to-all-start) | async-done | bytes 852000 | tf_op jit(solution)/shard_map/all_to_all | solution.py:378
  58.3 0.4 combine.1
  58.7 5.8 %collective-permute-start.4 = (f32[4,48,256]{2,1,0:T(8,128)S(1)}, f32[4,48,256]{2,1,0:T(8,128)S(1)}, u32[]{:S(2)}, u32[]{:S(2)}) collective-permute-start(f32[4,48,256]{2,1,0:T(8,128)S(1)} %combine.1), channel_id=1, source_target_pairs={{0,128},{128,0},{1,129},{129,1},{2,130},{130,2},{3,131},{131,3},{4... | collective-permute-start | bytes 589832 | tf_op jit(solution)/shard_map/ppermute | solution.py:389
  64.5 1.1 %collective-permute-done.4.total_ref = f32[4,48,256]{2,1,0:T(8,128)S(1)} collective-permute-done((f32[4,48,256]{2,1,0:T(8,128)S(1)}, f32[4,48,256]{2,1,0:T(8,128)S(1)}, u32[]{:S(2)}, u32[]{:S(2)}) %collective-permute-start.4) | collective-permute-done | bytes 196640 | tf_op jit(solution)/shard_map/ppermute | solution.py:389
  65.5 0.8 %finish.1 = (f32[16,48,256]{2,1,0:T(8,128)}, f32[4,48,256]{2,1,0:T(8,128)}) custom-call(f32[4,48,256]{2,1,0:T(8,128)S(1)} %collective-permute-done.4.total_ref, f32[4,48,256]{2,1,0:T(8,128)S(1)} %get-tuple-element.26.surface_ref, f32[48,256]{1,0:T(8,128)S(1)} %bitcast.16, f32[16,48,256]{2,1,0:T(8,128)} %aloft.1.aloft_ref), custom_call_target="tpu_custom_call", output_to_operand_aliasing={{0}: (3, {})} | custom-call | tf_op jit(solution)/shard_map/finish/pallas_call | solution.py:391
  (3 shorter events, 0.0 us)
Async XLA Ops:
  0.6 17.3 %copy-start.4 = (s32[1,192]{1,0:T(1,128)S(1)}, s32[1,192]{1,0:T(1,128)}, u32[]{:S(2)}) copy-start(s32[1,192]{1,0:T(1,128)} %source_ref.1) | copy-start | bytes 2308
  0.6 17.3 %copy-start.5 = (s32[1,192,1]{1,2,0:T(1,128)S(1)}, s32[1,192,1]{1,2,0:T(1,128)}, u32[]{:S(2)}) copy-start(s32[1,192,1]{1,2,0:T(1,128)} %param.13) | copy-start | bytes 2308
  0.7 17.3 %copy-start.6 = (s32[1,192]{1,0:T(1,128)S(1)}, s32[1,192]{1,0:T(1,128)}, u32[]{:S(2)}) copy-start(s32[1,192]{1,0:T(1,128)} %block_ref.1) | copy-start | bytes 2308
  1.7 11.0 %collective-permute-start = (f32[16,8,256]{2,1,0:T(8,128)S(1)}, f32[16,8,256]{2,1,0:T(8,128)S(1)}, u32[]{:S(2)}, u32[]{:S(2)}) collective-permute-start(f32[16,8,256]{2,1,0:T(8,128)S(1)} %get-tuple-element.31), channel_id=1, source_target_pairs={{0,16},{16,32},{32,48},{48,64},{64,80},{80,96},{96,112},{112,0},{1... | collective-permute-start | bytes 393224 | tf_op jit(solution)/shard_map/halo/ppermute | solution.py:290
  4.2 8.5 %collective-permute-start.1 = (f32[16,8,256]{2,1,0:T(8,128)S(1)}, f32[16,8,256]{2,1,0:T(8,128)S(1)}, u32[]{:S(2)}, u32[]{:S(2)}) collective-permute-start(f32[16,8,256]{2,1,0:T(8,128)S(1)} %get-tuple-element.30), channel_id=1, source_target_pairs={{0,112},{16,0},{32,16},{48,32},{64,48},{80,64},{96,80},{112,96},{1... | collective-permute-start | bytes 393224 | tf_op jit(solution)/shard_map/halo/ppermute | solution.py:291
  12.6 8.4 %copy-start = (f32[1,16,48,256]{3,2,1,0:T(8,128)S(1)}, f32[1,16,48,256]{3,2,1,0:T(8,128)}, u32[]{:S(2)}) copy-start(f32[1,16,48,256]{3,2,1,0:T(8,128)} %param.8) | copy-start | bytes 2359300
  12.6 8.4 %copy-start.2 = (f32[1,16]{1,0:T(1,128)S(1)}, f32[1,16]{1,0:T(1,128)}, u32[]{:S(2)}) copy-start(f32[1,16]{1,0:T(1,128)} %diffusion_ref.3) | copy-start | bytes 196
  12.7 8.4 %copy-start.3 = (f32[1,16]{1,0:T(1,128)S(1)}, f32[1,16]{1,0:T(1,128)}, u32[]{:S(2)}) copy-start(f32[1,16]{1,0:T(1,128)} %courant_ref.3) | copy-start | bytes 196
  12.8 8.2 %collective-permute-start.2 = (f32[64,128]{1,0:T(8,128)S(1)}, f32[64,128]{1,0:T(8,128)S(1)}, u32[]{:S(2)}, u32[]{:S(2)}) collective-permute-start(f32[64,128]{1,0:T(8,128)S(1)} %get-tuple-element.20), channel_id=1, source_target_pairs={{0,1},{1,2},{2,3},{3,4},{4,5},{5,6},{6,7},{7,8},{8,9},{9,10},{10,1... | collective-permute-start | bytes 98312 | tf_op jit(solution)/shard_map/halo/ppermute | solution.py:320
  14.1 6.9 %collective-permute-start.3 = (f32[64,128]{1,0:T(8,128)S(1)}, f32[64,128]{1,0:T(8,128)S(1)}, u32[]{:S(2)}, u32[]{:S(2)}) collective-permute-start(f32[64,128]{1,0:T(8,128)S(1)} %get-tuple-element.18.after_ref), channel_id=1, source_target_pairs={{0,15},{1,0},{2,1},{3,2},{4,3},{5,4},{6,5},{7,6},{8,7},{9,8},{10,9... | collective-permute-start | bytes 98312 | tf_op jit(solution)/shard_map/halo/ppermute | solution.py:319
  21.1 44.4 %copy-start.1 = (f32[1,48,256]{2,1,0:T(8,128)S(1)}, f32[1,48,256]{2,1,0:T(8,128)}, u32[]{:S(2)}) copy-start(f32[1,48,256]{2,1,0:T(8,128)} %param.11) | copy-start | bytes 147460
  25.7 32.6 %all-to-all-start = ((f32[128,13,1,128]{3,2,1,0:T(1,128)}), f32[128,13,1,128]{3,2,1,0:T(1,128)S(1)}, u32[]{:S(2)}, u32[]{:S(2)}) async-start(f32[128,13,1,128]{3,2,1,0:T(1,128)} %bitcast.6), calls=%async_computation | async-start | bytes 1703936 | tf_op jit(solution)/shard_map/all_to_all | solution.py:378
  58.7 6.8 %collective-permute-start.4 = (f32[4,48,256]{2,1,0:T(8,128)S(1)}, f32[4,48,256]{2,1,0:T(8,128)S(1)}, u32[]{:S(2)}, u32[]{:S(2)}) collective-permute-start(f32[4,48,256]{2,1,0:T(8,128)S(1)} %combine.1), channel_id=1, source_target_pairs={{0,128},{128,0},{1,129},{129,1},{2,130},{130,2},{3,131},{131,3},{4... | collective-permute-start | bytes 589832 | tf_op jit(solution)/shard_map/ppermute | solution.py:389

commit v6 on v5

--- a/solution.py
+++ b/solution.py
@@ -21,9 +21,9 @@
 CHUNK = 16
 N_CHUNKS = EPD // CHUNK
 ROWS_PER_PEER = CAP * NF + 1
-UNROLL = 28
-LATER = 5
-DEPTH = 4
+UNROLL = 24
+LATER = 6
+DEPTH = 5
 
 
 def ring(axis, shift):
@@ -332,7 +332,7 @@
             pltpu.VMEM((LATER * CHUNK, BLK, BLK), jnp.float32),
             pltpu.SemaphoreType.DMA((LATER,)),
         ],
-        compiler_params=limit(6),
+        compiler_params=limit(10),
         name="route",
     )(in_hbm(remap_weight[0]), src_block, dest_peer.reshape(1, EPD), dest_block, left)
 

time: 66.5 us -> 66.1 us (level)
  no operation moved by 1% of the time
where the time goes in v6:
time: 66.1 us; the launch traced here: 65.9 us
  starting transfers between devices  26.9 us (41%)
  waiting for transfers between devices  19.4 us (29%)
  Pallas kernels  17.7 us (27%)
  local copies, waits for them, and re-layouts  1.11 us (2%)
  between operations  0.76 us (1%)
    all_to_all x1, waiting for transfers between devices, body(): lax.all_to_all(outgoing.reshape(peers, ROWS_PER_PEER, 1, BLK), ('gx', 'gy...  18.3 us
    all_to_all x1, starting transfers between devices, body(): lax.all_to_all(outgoing.reshape(peers, ROWS_PER_PEER, 1, BLK), ('gx', 'gy...  9.48 us
    ppermute x1, starting transfers between devices, body(): total = lax.ppermute(total, 'sec', ring('sec', 1))  5.77 us
    pallas_call x1, Pallas kernels, body(): pl.pallas_call(surface_kernel, grid=(1,), in_specs=[smem, smem, smem, sme...  4.62 us
    pallas_call x1, Pallas kernels, body(): pl.pallas_call(aloft_kernel, grid=(LEV // NF - 1,), in_specs=[smem, smem,...  4.2 us
    ppermute x1, starting transfers between devices, body(): bottom = lax.ppermute(x[:, :HALO], 'gx', ring('gx', -1))  4.03 us
    pallas_call x1, Pallas kernels, body(): pl.pallas_call(prepare_kernel, in_specs=[anywhere] * 3, out_specs=[vmem]...  3.96 us
    ppermute x1, starting transfers between devices, body(): from_right = lax.ppermute(left, 'gy', ring('gy', -1))  3.81 us
  transfers between devices with their start and end apart: 6, of which 2 were waited for; matrix products, arithmetic and copies ran while one was open for 0% of the time, Pallas kernels for 18%

profile of v6, /device:TPU:1, one launch (start us, length us, event | category | flops | bytes accessed | tf_op | source)
XLA Modules:
  0.0 65.9 jit_solution(10008696243729771945)
XLA Ops:
  0.6 1.0 %fusion = (f32[16,8,256]{2,1,0:T(8,128)S(1)}, f32[16,8,256]{2,1,0:T(8,128)S(1)}) fusion(f32[16,48,256]{2,1,0:T(8,128)} %bitcast.11), kind=kLoop, calls=%fused_computation | loop fusion | bytes 524288 | tf_op jit(solution)/shard_map/halo/slice | solution.py:291
  1.6 2.5 %collective-permute-start = (f32[16,8,256]{2,1,0:T(8,128)S(1)}, f32[16,8,256]{2,1,0:T(8,128)S(1)}, u32[]{:S(2)}, u32[]{:S(2)}) collective-permute-start(f32[16,8,256]{2,1,0:T(8,128)S(1)} %get-tuple-element.31), channel_id=1, source_target_pairs={{0,16},{16,32},{32,48},{48,64},{64,80},{80,96},{96,112},{112,0},{1... | collective-permute-start | bytes 393224 | tf_op jit(solution)/shard_map/halo/ppermute | solution.py:290
  4.2 4.0 %collective-permute-start.1 = (f32[16,8,256]{2,1,0:T(8,128)S(1)}, f32[16,8,256]{2,1,0:T(8,128)S(1)}, u32[]{:S(2)}, u32[]{:S(2)}) collective-permute-start(f32[16,8,256]{2,1,0:T(8,128)S(1)} %get-tuple-element.30), channel_id=1, source_target_pairs={{0,112},{16,0},{32,16},{48,32},{64,48},{80,64},{96,80},{112,96},{1... | collective-permute-start | bytes 393224 | tf_op jit(solution)/shard_map/halo/ppermute | solution.py:291
  8.2 0.1 stack.15.meta_ref
  8.3 0.0 copy-start.4
  8.3 4.0 %prepare.1 = (bf16[48,256,256]{2,1,0:T(8,128)(2,1)S(1)}, f32[48,128]{1,0:T(8,128)S(1)}, f32[48,128]{1,0:T(8,128)S(1)}) custom-call(f32[192,128,128]{2,1,0:T(8,128)} %bitcast.18, f32[16,48,256]{2,1,0:T(8,128)} %bitcast.12, s32[5]{0:T(128)S(1)} %stack.15.meta_ref), custom_call_target="tpu_custom_call" | custom-call | tf_op jit(solution)/shard_map/prepare/prepare/pallas_call | solution.py:295
  12.2 0.0 collective-permute-done.top_ref
  12.3 0.0 collective-permute-done.1.bottom_ref
  12.3 0.1 pack.1
  12.4 1.3 %collective-permute-start.2 = (f32[64,128]{1,0:T(8,128)S(1)}, f32[64,128]{1,0:T(8,128)S(1)}, u32[]{:S(2)}, u32[]{:S(2)}) collective-permute-start(f32[64,128]{1,0:T(8,128)S(1)} %get-tuple-element.20), channel_id=1, source_target_pairs={{0,1},{1,2},{2,3},{3,4},{4,5},{5,6},{6,7},{7,8},{8,9},{9,10},{10,1... | collective-permute-start | bytes 98312 | tf_op jit(solution)/shard_map/halo/ppermute | solution.py:320
  13.7 3.8 %collective-permute-start.3 = (f32[64,128]{1,0:T(8,128)S(1)}, f32[64,128]{1,0:T(8,128)S(1)}, u32[]{:S(2)}, u32[]{:S(2)}) collective-permute-start(f32[64,128]{1,0:T(8,128)S(1)} %get-tuple-element.18.after_ref), channel_id=1, source_target_pairs={{0,15},{1,0},{2,1},{3,2},{4,3},{5,4},{6,5},{7,6},{8,7},{9,8},{10,9... | collective-permute-start | bytes 98312 | tf_op jit(solution)/shard_map/halo/ppermute | solution.py:319
  17.5 0.0 copy-done.4
  17.5 0.0 copy-done.5
  17.5 0.0 copy-done.6
  17.5 0.0 copy-start.2
  17.5 0.0 copy-start.3
  17.5 3.7 %route.1 = (bf16[48,256,256]{2,1,0:T(8,128)(2,1)S(1)}, s32[2,192]{1,0:T(2,128)S(1)}, f32[128,128]{1,0:T(8,128)S(1)}) custom-call(f32[192,128,128]{2,1,0:T(8,128)} %bitcast.19, s32[1,192]{1,0:T(1,128)S(1)} %copy-done.4, s32[1,192]{1,0:T(1,128)S(1)} %bitcast.17, s32[1,192]{1,0:T(1,128)S(1)} %copy-done.6, f32[64,128]{1,0:T(8,128)S(1)} %get-tuple-element.18.after_ref), custom_call_target="tpu_custom_call" | custom-call | tf_op jit(solution)/shard_map/route/pallas_call | solution.py:322
  21.2 0.0 collective-permute-done.2.left_ref
  21.2 0.0 collective-permute-done.3.right_ref
  21.2 0.0 copy-done
  21.2 0.0 copy-done.2
  21.2 0.0 copy-done.3
  21.3 0.0 copy-start.1
  21.3 4.6 %surface.1 = (f32[1664,128]{1,0:T(8,128)}, f32[4,48,256]{2,1,0:T(8,128)S(1)}) custom-call(s32[5]{0:T(128)S(1)} %stack.15.meta_ref, f32[1,16]{1,0:T(1,128)S(1)} %copy-done.2, f32[1,16]{1,0:T(1,128)S(1)} %copy-done.3, s32[2,192]{1,0:T(2,128)S(1)} %get-tuple-element.19.route_ref, f32[16,48,256]{2,1,0:T(8,128)S(1)} %bitcast.13, ...), custom_call_target="tpu_custom_call" | custom-call | tf_op jit(solution)/shard_map/surface/pallas_call | solution.py:342
  25.9 9.5 %all-to-all-start = ((f32[128,13,1,128]{3,2,1,0:T(1,128)}), f32[128,13,1,128]{3,2,1,0:T(1,128)S(1)}, u32[]{:S(2)}, u32[]{:S(2)}) async-start(f32[128,13,1,128]{3,2,1,0:T(1,128)} %bitcast.6), calls=%async_computation | async-start | bytes 1703936 | tf_op jit(solution)/shard_map/all_to_all | solution.py:378
  35.4 4.2 %aloft.1.aloft_ref = f32[16,48,256]{2,1,0:T(8,128)} custom-call(s32[5]{0:T(128)S(1)} %stack.15.meta_ref, f32[1,16]{1,0:T(1,128)S(1)} %copy-done.2, f32[1,16]{1,0:T(1,128)S(1)} %copy-done.3, f32[16,48,256]{2,1,0:T(8,128)S(1)} %bitcast.14, f32[16,8,256]{2,1,0:T(8,128)S(1)} %collective-permute-done.top_ref, ...), custom_call_target="tpu_custom_call" | custom-call | tf_op jit(solution)/shard_map/aloft/pallas_call | solution.py:367
  39.6 18.3 %all-to-all-done = f32[128,13,1,128]{3,2,1,0:T(1,128)S(1)} async-done(((f32[128,13,1,128]{3,2,1,0:T(1,128)}), f32[128,13,1,128]{3,2,1,0:T(1,128)S(1)}, u32[]{:S(2)}, u32[]{:S(2)}) %all-to-all-start) | async-done | bytes 852000 | tf_op jit(solution)/shard_map/all_to_all | solution.py:378
  57.9 0.4 combine.1
  58.3 5.8 %collective-permute-start.4 = (f32[4,48,256]{2,1,0:T(8,128)S(1)}, f32[4,48,256]{2,1,0:T(8,128)S(1)}, u32[]{:S(2)}, u32[]{:S(2)}) collective-permute-start(f32[4,48,256]{2,1,0:T(8,128)S(1)} %combine.1), channel_id=1, source_target_pairs={{0,128},{128,0},{1,129},{129,1},{2,130},{130,2},{3,131},{131,3},{4... | collective-permute-start | bytes 589832 | tf_op jit(solution)/shard_map/ppermute | solution.py:389
  64.0 1.1 %collective-permute-done.4.total_ref = f32[4,48,256]{2,1,0:T(8,128)S(1)} collective-permute-done((f32[4,48,256]{2,1,0:T(8,128)S(1)}, f32[4,48,256]{2,1,0:T(8,128)S(1)}, u32[]{:S(2)}, u32[]{:S(2)}) %collective-permute-start.4) | collective-permute-done | bytes 196640 | tf_op jit(solution)/shard_map/ppermute | solution.py:389
  65.1 0.0 copy-done.1
  65.1 0.8 %finish.1 = (f32[16,48,256]{2,1,0:T(8,128)}, f32[4,48,256]{2,1,0:T(8,128)}) custom-call(f32[4,48,256]{2,1,0:T(8,128)S(1)} %collective-permute-done.4.total_ref, f32[4,48,256]{2,1,0:T(8,128)S(1)} %get-tuple-element.26.surface_ref, f32[48,256]{1,0:T(8,128)S(1)} %bitcast.16, f32[16,48,256]{2,1,0:T(8,128)} %aloft.1.aloft_ref), custom_call_target="tpu_custom_call", output_to_operand_aliasing={{0}: (3, {})} | custom-call | tf_op jit(solution)/shard_map/finish/pallas_call | solution.py:391
  (3 shorter events, 0.0 us)
Async XLA Ops:
  1.6 10.6 %collective-permute-start = (f32[16,8,256]{2,1,0:T(8,128)S(1)}, f32[16,8,256]{2,1,0:T(8,128)S(1)}, u32[]{:S(2)}, u32[]{:S(2)}) collective-permute-start(f32[16,8,256]{2,1,0:T(8,128)S(1)} %get-tuple-element.31), channel_id=1, source_target_pairs={{0,16},{16,32},{32,48},{48,64},{64,80},{80,96},{96,112},{112,0},{1... | collective-permute-start | bytes 393224 | tf_op jit(solution)/shard_map/halo/ppermute | solution.py:290
  4.2 8.1 %collective-permute-start.1 = (f32[16,8,256]{2,1,0:T(8,128)S(1)}, f32[16,8,256]{2,1,0:T(8,128)S(1)}, u32[]{:S(2)}, u32[]{:S(2)}) collective-permute-start(f32[16,8,256]{2,1,0:T(8,128)S(1)} %get-tuple-element.30), channel_id=1, source_target_pairs={{0,112},{16,0},{32,16},{48,32},{64,48},{80,64},{96,80},{112,96},{1... | collective-permute-start | bytes 393224 | tf_op jit(solution)/shard_map/halo/ppermute | solution.py:291
  8.3 9.2 %copy-start.4 = (s32[1,192]{1,0:T(1,128)S(1)}, s32[1,192]{1,0:T(1,128)}, u32[]{:S(2)}) copy-start(s32[1,192]{1,0:T(1,128)} %source_ref.1) | copy-start | bytes 2308
  8.3 9.2 %copy-start.5 = (s32[1,192,1]{1,2,0:T(1,128)S(1)}, s32[1,192,1]{1,2,0:T(1,128)}, u32[]{:S(2)}) copy-start(s32[1,192,1]{1,2,0:T(1,128)} %param.13) | copy-start | bytes 2308
  8.3 9.2 %copy-start.6 = (s32[1,192]{1,0:T(1,128)S(1)}, s32[1,192]{1,0:T(1,128)}, u32[]{:S(2)}) copy-start(s32[1,192]{1,0:T(1,128)} %block_ref.1) | copy-start | bytes 2308
  12.4 8.8 %collective-permute-start.2 = (f32[64,128]{1,0:T(8,128)S(1)}, f32[64,128]{1,0:T(8,128)S(1)}, u32[]{:S(2)}, u32[]{:S(2)}) collective-permute-start(f32[64,128]{1,0:T(8,128)S(1)} %get-tuple-element.20), channel_id=1, source_target_pairs={{0,1},{1,2},{2,3},{3,4},{4,5},{5,6},{6,7},{7,8},{8,9},{9,10},{10,1... | collective-permute-start | bytes 98312 | tf_op jit(solution)/shard_map/halo/ppermute | solution.py:320
  13.7 7.5 %collective-permute-start.3 = (f32[64,128]{1,0:T(8,128)S(1)}, f32[64,128]{1,0:T(8,128)S(1)}, u32[]{:S(2)}, u32[]{:S(2)}) collective-permute-start(f32[64,128]{1,0:T(8,128)S(1)} %get-tuple-element.18.after_ref), channel_id=1, source_target_pairs={{0,15},{1,0},{2,1},{3,2},{4,3},{5,4},{6,5},{7,6},{8,7},{9,8},{10,9... | collective-permute-start | bytes 98312 | tf_op jit(solution)/shard_map/halo/ppermute | solution.py:319
  17.5 3.7 %copy-start = (f32[1,16,48,256]{3,2,1,0:T(8,128)S(1)}, f32[1,16,48,256]{3,2,1,0:T(8,128)}, u32[]{:S(2)}) copy-start(f32[1,16,48,256]{3,2,1,0:T(8,128)} %param.8) | copy-start | bytes 2359300
  17.5 3.7 %copy-start.2 = (f32[1,16]{1,0:T(1,128)S(1)}, f32[1,16]{1,0:T(1,128)}, u32[]{:S(2)}) copy-start(f32[1,16]{1,0:T(1,128)} %diffusion_ref.3) | copy-start | bytes 196
  17.5 3.7 %copy-start.3 = (f32[1,16]{1,0:T(1,128)S(1)}, f32[1,16]{1,0:T(1,128)}, u32[]{:S(2)}) copy-start(f32[1,16]{1,0:T(1,128)} %courant_ref.3) | copy-start | bytes 196
  21.3 43.9 %copy-start.1 = (f32[1,48,256]{2,1,0:T(8,128)S(1)}, f32[1,48,256]{2,1,0:T(8,128)}, u32[]{:S(2)}) copy-start(f32[1,48,256]{2,1,0:T(8,128)} %param.11) | copy-start | bytes 147460
  25.9 32.0 %all-to-all-start = ((f32[128,13,1,128]{3,2,1,0:T(1,128)}), f32[128,13,1,128]{3,2,1,0:T(1,128)S(1)}, u32[]{:S(2)}, u32[]{:S(2)}) async-start(f32[128,13,1,128]{3,2,1,0:T(1,128)} %bitcast.6), calls=%async_computation | async-start | bytes 1703936 | tf_op jit(solution)/shard_map/all_to_all | solution.py:378
  58.3 6.8 %collective-permute-start.4 = (f32[4,48,256]{2,1,0:T(8,128)S(1)}, f32[4,48,256]{2,1,0:T(8,128)S(1)}, u32[]{:S(2)}, u32[]{:S(2)}) collective-permute-start(f32[4,48,256]{2,1,0:T(8,128)S(1)} %combine.1), channel_id=1, source_target_pairs={{0,128},{128,0},{1,129},{129,1},{2,130},{130,2},{3,131},{131,3},{4... | collective-permute-start | bytes 589832 | tf_op jit(solution)/shard_map/ppermute | solution.py:389
